TPU v7x, 256 devices: a whole 4x4x8 slice. The times are simulated.
256 devices in a mesh: child: 8 (over x, core), row: 8 (over z), col: 4 (over y).
Axes of the slice: x: 4, y: 4, z: 8, core: 2. Of those that a mesh axis runs over, the one named last changes fastest.
Arguments:
- schur_blocks: bfloat16 [8, 8192, 8192], P('child', 'row', 'col'), may hold values from -0.0625 to 0.0625
- sketch_cols: bfloat16 [8192, 256], P('row'), may hold values from -6 to 6
- block_map: int32 [8, 64], replicated, may hold values from 0 to 255, as said below
- owner_slot: int32 [32], replicated, may hold values from 0 to 15, as said below
Outputs:
- basis_out: float32 [16, 8, 1024, 256], P('child', 'row', 'col')
- coupling_out: float32 [16, 8, 256, 256], P('child', 'row', 'col')
Inputs may be any that keep to these rules, and one draw needn't show every extreme that they name: `block_map`: entry [c, j] keeps the block's place in its group (entry % 8 == j % 8) and lies at the row position of the child's group: (entry // 8) // 4 == (j // 8). The entries of one child are distinct. Of the blocks of one child with equal (j // 8), at most 4 land in groups whose owner_slot // 2 is equal, and in every draw exactly 4 do for one owner. Group g belongs to owner owner_slot[g] // 2. Groups with equal g // 4 have distinct slots, and at every row position some owner holds 2 groups.
All inputs are finite; a program needn't handle non-finite values.
Results may differ from a plain program's by a relative error of at most 0.017.
Values may be sent and summed in bfloat16 or wider, within the bound.
A program may use at most 64 MiB of HBM per device.

v0:
```python
import jax
import jax.numpy as jnp
from jax import lax
from jax.sharding import PartitionSpec as P

SKETCH = 256
BLOCK = 128
GROUP = 1024
SLOTS = 2


gram_shift = 64.0
highest = lax.Precision.HIGHEST


def split_up(value, dim, peers):
    shape = value.shape
    tiles = value.reshape(*shape[:dim], peers, shape[dim] // peers, *shape[dim + 1 :])
    return jnp.moveaxis(tiles, dim, 0)


def sum_at_owner(value, axis, dim):
    tiles = split_up(value, dim, lax.axis_size(axis))
    arrived = lax.all_to_all(tiles, axis, split_axis=0, concat_axis=0, tiled=True)
    return arrived.sum(axis=0)


def sent_to_all(value, axis):
    copies = jnp.broadcast_to(value, (lax.axis_size(axis), *value.shape))
    return lax.all_to_all(copies, axis, split_axis=0, concat_axis=0, tiled=True)


def taken_together(value, axis):
    everything = sent_to_all(value, axis)
    return jnp.sum(everything, axis=0)


def gather_axes(value, axes, dim):
    for axis in reversed(axes):
        value = lax.all_gather(value, axis, axis=dim, tiled=True)
    return value


def sum_at_owner_2(value, axis, dim):
    peers = lax.axis_size(axis)
    tiles = lax.all_to_all(split_up(value, dim, peers), axis, 0, 0, tiled=True)
    return jnp.sum(tiles.astype(jnp.float32), axis=0)


def rank_within(owners, total):
    onehot = (owners[..., None] == jnp.arange(total, dtype=jnp.int32)).astype(jnp.int32)
    before = jnp.cumsum(onehot, axis=-2) - onehot
    return jnp.sum(before * onehot, axis=-1)


def one_hot(indices, total, dtype):
    return (indices[..., None] == jnp.arange(total, dtype=jnp.int32)).astype(dtype)


def slot_table(block_map, owner_slot):
    groups = block_map // (GROUP // BLOCK)
    matches = groups[..., None] == jnp.arange(owner_slot.shape[0], dtype=jnp.int32)
    return jnp.sum(jnp.where(matches, owner_slot, 0), axis=-1)


def transposed_product(left, right):
    return lax.dot_general(
        left, right, (((0,), (0,)), ((), ())), preferred_element_type=jnp.float32
    )


def shards(schur_blocks, sketch_cols, block_map, owner_slot):
    children = lax.axis_size("child")
    row_count = lax.axis_size("row")
    col_count = lax.axis_size("col")
    member = lax.axis_index("child")
    row_index = lax.axis_index("row")
    col_index = lax.axis_index("col")
    matrix = schur_blocks[0]
    own_rows = matrix.shape[0]
    own_cols = matrix.shape[1]
    offsets = GROUP // BLOCK
    per_row = own_rows // GROUP
    off_col = offsets // col_count
    held_blocks = per_row * offsets
    back_cap = per_row * off_col
    share_rows = SKETCH // col_count
    row_slots = lax.dynamic_slice_in_dim(
        slot_table(block_map, owner_slot), row_index * held_blocks, held_blocks, 1
    )
    slot_grid = row_slots.reshape(children, per_row, offsets)
    back_slots = lax.dynamic_slice_in_dim(slot_grid, col_index * off_col, off_col, 2).reshape(
        children, back_cap
    )
    back_owner = back_slots // SLOTS
    back_rank = rank_within(back_owner, children)
    source_index = (
        back_slots % SLOTS * off_col + (jnp.arange(back_cap, dtype=jnp.int32) % off_col)[None, :]
    )
    position = jnp.arange(children, dtype=jnp.int32)[:, None] * back_cap + back_rank
    send_mask = (back_owner == member).astype(jnp.float32)
    to_position = one_hot(position, children * back_cap, jnp.float32) * send_mask[..., None]
    from_source = one_hot(source_index, SLOTS * off_col, jnp.float32)
    route_table = jnp.einsum("ckp,ckq->pq", to_position, from_source)
    my_owner = lax.dynamic_index_in_dim(back_owner, member, 0, keepdims=False)
    my_rank = lax.dynamic_index_in_dim(back_rank, member, 0, keepdims=False)
    pick_table = one_hot(my_owner * back_cap + my_rank, children * back_cap, jnp.float32)
    power_cols = lax.psum(transposed_product(matrix, sketch_cols), "row").astype(jnp.bfloat16)
    sample_part = jnp.dot(matrix, power_cols, preferred_element_type=jnp.float32).reshape(
        held_blocks, BLOCK, SKETCH
    )
    summed = sum_at_owner(sample_part.reshape(per_row, offsets, BLOCK, SKETCH), "col", 1)
    outgoing = jnp.einsum(
        "mp,mxr->pxr", pick_table, summed.reshape(back_cap, BLOCK, SKETCH), precision=highest
    )
    landed = lax.all_to_all(outgoing, "child", split_axis=0, concat_axis=0, tiled=True)
    parent_rows = jnp.einsum("pq,pxr->qxr", route_table, landed, precision=highest)
    stacked = parent_rows.reshape(SLOTS, off_col * BLOCK, SKETCH)
    gram_part = jnp.einsum("snr,snq->srq", stacked, stacked, precision=highest)
    gram_matrix = taken_together(gram_part, "col") + gram_shift * jnp.eye(SKETCH, dtype=jnp.float32)
    factor = jnp.linalg.cholesky(gram_matrix)
    basis_rows = jnp.swapaxes(
        jax.scipy.linalg.solve_triangular(factor, jnp.swapaxes(stacked, 1, 2), lower=True), 1, 2
    )
    rounded = basis_rows.astype(jnp.bfloat16)
    route_back = route_table.astype(jnp.bfloat16)
    back_buffer = jnp.einsum(
        "pq,qxr->pxr",
        route_back,
        rounded.reshape(SLOTS * off_col, BLOCK, SKETCH),
        preferred_element_type=jnp.float32,
    ).astype(jnp.bfloat16)
    returned = lax.all_to_all(back_buffer, "child", split_axis=0, concat_axis=0, tiled=True)
    pick_back = pick_table.astype(jnp.bfloat16)
    child_part = jnp.einsum(
        "mp,pxr->mxr", pick_back, returned, preferred_element_type=jnp.float32
    ).astype(jnp.bfloat16)
    gathered = gather_axes(child_part, ("row", "col"), 0)
    child_basis = gathered.reshape(row_count, col_count, per_row, off_col, BLOCK, SKETCH)
    child_basis = child_basis.transpose(0, 2, 1, 3, 4, 5).reshape(row_count * own_rows, SKETCH)
    column_basis = lax.dynamic_slice_in_dim(child_basis, col_index * own_cols, own_cols, 0)
    weighted = jnp.dot(matrix, column_basis, preferred_element_type=jnp.float32).reshape(
        held_blocks, BLOCK, SKETCH
    )
    row_basis = lax.dynamic_slice_in_dim(child_basis, row_index * own_rows, own_rows, 0).reshape(
        held_blocks, BLOCK, SKETCH
    )
    projected = jnp.einsum(
        "bxr,bxs->brs", row_basis.astype(jnp.float32), weighted, precision=highest
    )
    my_slots = lax.dynamic_index_in_dim(row_slots, member, 0, keepdims=False)
    slot_pick = one_hot(my_slots, children * SLOTS, jnp.float32)
    by_slot = jnp.einsum("bt,brs->trs", slot_pick, projected, precision=highest)
    arranged = by_slot.reshape(children, SLOTS, col_count, share_rows, SKETCH).transpose(
        0, 2, 1, 3, 4
    )
    arranged = arranged.reshape(children * col_count * SLOTS * share_rows, SKETCH)
    coupling = sum_at_owner_2(arranged.astype(jnp.bfloat16), ("child", "col"), 0).reshape(
        SLOTS, share_rows, SKETCH
    )
    return (
        basis_rows.reshape(SLOTS, 1, off_col * BLOCK, SKETCH),
        coupling.reshape(SLOTS, 1, share_rows, SKETCH),
    )


def solution(mesh):
    placed = (P("child", "row", "col"), P("row", None), P(), P())
    return jax.shard_map(
        shards,
        mesh=mesh,
        in_specs=placed,
        out_specs=(P("child", "row", "col", None), P("child", "row", "col", None)),
        check_vma=False,
    )
```

profile of v0, /device:TPU:1, one launch (start us, length us, event | category | flops | bytes accessed | tf_op | source)
XLA Modules:
  0.0 433.1 jit_solution(4125545020065490564)
XLA Ops:
  7.2 1.0 copy-done
  8.2 3.5 fusion.4
  11.7 59.9 %all-reduce.2 = bf16[2048,256]{1,0:T(8,128)(2,1)} all-reduce(f32[2048,256]{1,0:T(8,128)S(1)} %fusion.4), channel_id=1, replica_groups=mesh['child'=8,'row'=8,'col'=4] {'row'}, use_global_device_ids=true, to_apply=%region_3.4 | all-reduce | flops 524288 | bytes 3145728 | tf_op jit(solution)/shard_map/psum | solution.py:108
  71.6 3.8 fusion.13
  75.4 0.9 transpose_reshape_reshape_reshape.3
  76.3 1.4 copy.122
  77.7 4.2 all-to-all-start
  82.6 9.0 %all-to-all-done = f32[4,1,2,128,256]{3,2,4,1,0:T(2,128)S(1)} async-done(((f32[4,1,2,128,256]{3,2,4,1,0:T(2,128)}), f32[4,1,2,128,256]{3,2,4,1,0:T(2,128)S(1)}, u32[]{:S(2)}, u32[]{:S(2)}) %all-to-all-start) | async-done | bytes 1048608 | tf_op jit(solution)/shard_map/all_to_all | solution.py:24
  91.6 0.6 reduce_sum.49
  92.4 1.2 fusion.53
  93.5 2.6 copy.125
  96.1 16.0 %all-to-all-start.1 = ((f32[16,128,256]{2,1,0:T(8,128)}), f32[16,128,256]{2,1,0:T(8,128)S(1)}, u32[]{:S(2)}, u32[]{:S(2)}) async-start(f32[16,128,256]{2,1,0:T(8,128)} %copy.125), calls=%async_computation.1 | async-start | bytes 4194304 | tf_op jit(solution)/shard_map/all_to_all | solution.py:116
  112.5 25.8 %all-to-all-done.1 = f32[16,128,256]{2,1,0:T(8,128)S(1)} async-done(((f32[16,128,256]{2,1,0:T(8,128)}), f32[16,128,256]{2,1,0:T(8,128)S(1)}, u32[]{:S(2)}, u32[]{:S(2)}) %all-to-all-start.1) | async-done | bytes 2097184 | tf_op jit(solution)/shard_map/all_to_all | solution.py:116
  138.3 2.2 fusion.8
  140.7 1.1 fusion.69
  141.8 1.5 broadcast_in_dim.14
  143.3 3.6 all-to-all-start.2
  147.2 0.7 fusion.29
  148.0 1.0 copy.133
  149.0 23.4 %all-to-all-done.2 = f32[4,2,256,256]{3,2,1,0:T(8,128)S(1)} async-done(((f32[4,2,256,256]{3,2,1,0:T(8,128)}), f32[4,2,256,256]{3,2,1,0:T(8,128)S(1)}, u32[]{:S(2)}, u32[]{:S(2)}) %all-to-all-start.2) | async-done | bytes 2097184 | tf_op jit(solution)/shard_map/all_to_all | solution.py:30
  172.7 1.1 fusion.24
  173.8 23.5 %custom-call.17 = f32[2,128,128]{2,1,0:T(8,128)S(1)} custom-call(f32[2,128,128]{2,1,0:T(8,128)S(1)} %cholesky.122), custom_call_target="Cholesky" | custom-call | tf_op jit(solution)/shard_map/jit(cholesky)/cholesky | solution.py:121
  197.3 19.7 %custom-call.18 = f32[2,1,128,128]{2,3,1,0:T(8,128)S(1)} custom-call(f32[2,1,128,128]{3,2,1,0:T(8,128)S(1)} %select_bitcast_fusion), custom_call_target="InvertDiagBlocksLowerTriangular" | custom-call | tf_op jit(solution)/shard_map/jit(cholesky)/cholesky | solution.py:121
  217.7 23.5 %custom-call.19 = f32[2,128,128]{2,1,0:T(8,128)S(1)} custom-call(f32[2,128,128]{2,1,0:T(8,128)S(1)} %convolution_subtract_fusion.1), custom_call_target="Cholesky" | custom-call | tf_op jit(solution)/shard_map/jit(cholesky)/cholesky | solution.py:121
  241.6 5.4 %while.1 = (s32[]{:T(128)}, f32[2,256,256]{2,1,0:T(8,128)S(1)}, s32[2,2]{1,0:T(2,128)S(1)}, f32[2,2,128,128]{3,2,0,1:T(8,128)}, s32[]{:T(128)}) while((s32[]{:T(128)}, f32[2,256,256]{2,1,0:T(8,128)S(1)}, s32[2,2]{1,0:T(2,128)S(1)}, f32[2,2,128,128]{3,2,0,1:T(8,128)}, s32[]{:T(128)}) %tuple.35), condition=%wide.while_cond, body=%wide.while_body.sunk | while | flops 2 | bytes 263277 | solution.py:123
  241.6 0.7 fusion.84
  242.3 2.0 bitcast_dynamic-update-slice_fusion.2
  244.3 0.7 fusion.84
  245.0 2.0 bitcast_dynamic-update-slice_fusion.2
  247.0 40.1 %custom-call.20 = f32[2,2,128,128]{2,3,1,0:T(8,128)S(1)} custom-call(f32[2,2,128,128]{3,2,1,0:T(8,128)} %bitcast.112), custom_call_target="InvertDiagBlocksLowerTriangular" | custom-call | tf_op jit(solution)/shard_map/jit(_solve_triangular)/vmap()/triangular_solve | solution.py:123
  287.9 0.4 fusion.32
  288.6 0.5 convolution_convert_fusion
  289.4 19.2 %all_to_all.25 = bf16[16,128,256]{2,1,0:T(8,128)(2,1)S(1)} all-to-all(bf16[16,128,256]{2,1,0:T(8,128)(2,1)S(1)} %copy.138), channel_id=1, replica_groups=mesh['child'=8,'row'=8,'col'=4] {'child'}, dimensions={0} | all-to-all | bytes 2097152 | tf_op jit(solution)/shard_map/all_to_all | solution.py:133
  308.6 0.7 convolution_convert_fusion.1
  309.3 10.6 %all_gather.6 = bf16[8,128,256]{2,1,0:T(8,128)(2,1)} all-gather(bf16[2,128,256]{2,1,0:T(8,128)(2,1)S(1)} %copy.140), channel_id=1, replica_groups=mesh['child'=8,'row'=8,'col'=4] {'col'}, dimensions={0}, use_global_device_ids=true | all-gather | bytes 655360 | tf_op jit(solution)/shard_map/all_gather | solution.py:40
  320.1 53.4 %all-gather.2.cloned.1.call-done = bf16[64,128,256]{2,1,0:T(8,128)(2,1)} async-done(((bf16[8,128,256]{2,1,0:T(8,128)(2,1)}), bf16[64,128,256]{2,1,0:T(8,128)(2,1)}) %all-gather.2.cloned.1.call-update) | async-done | bytes 4194320 | tf_op jit(solution)/shard_map/all_gather | solution.py:40
  373.5 1.1 constant_dynamic-slice_fusion.1
  374.5 4.8 %fusion.16 = f32[1024,256]{0,1:T(8,128)} fusion(bf16[1,1024,2048]{2,1,0:T(8,128)(2,1)} %param.4, bf16[8192,256]{1,0:T(8,128)(2,1)} %bitcast.111, s32[]{:T(128)S(6)} %select_n.73), kind=kOutput, calls=%fused_computation.16 | convolution fusion | flops 1073741824 | bytes 6291460 | tf_op jit(solution)/shard_map/dot_general | solution.py:142
  379.3 1.6 copy.151
  380.9 1.1 fusion.70
  382.0 2.7 fusion.10
  384.7 2.2 convert_element_type.58
  386.9 3.7 copy.144
  390.6 7.7 %all-to-all-start.4 = ((bf16[32,128,256]{2,1,0:T(8,128)(2,1)}), bf16[32,128,256]{2,1,0:T(8,128)(2,1)S(1)}, u32[]{:S(2)}, u32[]{:S(2)}) async-start(bf16[32,128,256]{2,1,0:T(8,128)(2,1)} %bitcast.103), calls=%async_computation.4 | async-start | bytes 4194304 | tf_op jit(solution)/shard_map/all_to_all | solution.py:46
  398.3 0.8 fusion.25
  399.1 2.0 copy.145
  401.2 24.2 %all-to-all-done.4 = bf16[32,128,256]{2,1,0:T(8,128)(2,1)S(1)} async-done(((bf16[32,128,256]{2,1,0:T(8,128)(2,1)}), bf16[32,128,256]{2,1,0:T(8,128)(2,1)S(1)}, u32[]{:S(2)}, u32[]{:S(2)}) %all-to-all-start.4) | async-done | bytes 2097184 | tf_op jit(solution)/shard_map/all_to_all | solution.py:46
  425.3 0.9 convert_reduce_fusion
  (53 shorter events, 4.7 us)
Async XLA Ops:
  7.2 1.0 copy-start
  76.3 5.5 %copy-start.2 = (s32[8,64]{1,0:T(8,128)S(1)}, s32[8,64]{1,0:T(8,128)}, u32[]{:S(2)}) copy-start(s32[8,64]{1,0:T(8,128)} %param.6) | copy-start | bytes 6148
  76.3 5.6 %copy-start.3 = (s32[32]{0:T(128)S(1)}, s32[32]{0:T(128)}, u32[]{:S(2)}) copy-start(s32[32]{0:T(128)} %param.7) | copy-start | bytes 388
  77.7 13.9 %all-to-all-start = ((f32[4,1,2,128,256]{3,2,4,1,0:T(2,128)}), f32[4,1,2,128,256]{3,2,4,1,0:T(2,128)S(1)}, u32[]{:S(2)}, u32[]{:S(2)}) async-start(f32[4,1,2,128,256]{3,2,4,1,0:T(2,128)} %copy.122), calls=%async_computation | async-start | bytes 2097152 | tf_op jit(solution)/shard_map/all_to_all | solution.py:24
  96.1 42.2 %all-to-all-start.1 = ((f32[16,128,256]{2,1,0:T(8,128)}), f32[16,128,256]{2,1,0:T(8,128)S(1)}, u32[]{:S(2)}, u32[]{:S(2)}) async-start(f32[16,128,256]{2,1,0:T(8,128)} %copy.125), calls=%async_computation.1 | async-start | bytes 4194304 | tf_op jit(solution)/shard_map/all_to_all | solution.py:116
  143.3 29.0 %all-to-all-start.2 = ((f32[4,2,256,256]{3,2,1,0:T(8,128)}), f32[4,2,256,256]{3,2,1,0:T(8,128)S(1)}, u32[]{:S(2)}, u32[]{:S(2)}) async-start(f32[4,2,256,256]{3,2,1,0:T(8,128)} %broadcast_in_dim.14), calls=%async_computation.2 | async-start | bytes 4194304 | tf_op jit(solution)/shard_map/all_to_all | solution.py:30
  146.9 226.6 %all-gather.2.cloned.1.call-start = ((), (), s32[]{:S(2)}) async-start(), calls=%async_computation.5 | async-start | bytes 4718592 | tf_op jit(solution)/shard_map/all_gather | solution.py:40
  197.3 89.8 %copy-start.1 = (f32[2,256,256]{1,2,0:T(8,128)S(1)}, f32[2,256,256]{1,2,0:T(8,128)}, u32[]{:S(2)}) copy-start(f32[2,256,256]{1,2,0:T(8,128)} %copy.133) | copy-start | bytes 1572868
  390.6 34.8 %all-to-all-start.4 = ((bf16[32,128,256]{2,1,0:T(8,128)(2,1)}), bf16[32,128,256]{2,1,0:T(8,128)(2,1)S(1)}, u32[]{:S(2)}, u32[]{:S(2)}) async-start(bf16[32,128,256]{2,1,0:T(8,128)(2,1)} %bitcast.103), calls=%async_computation.4 | async-start | bytes 4194304 | tf_op jit(solution)/shard_map/all_to_all | solution.py:46
Sparse Core Ops, SparseCore 0:
  320.1 53.3 all-gather.1
where the time goes:
time: 434 us; the launch traced here: 433 us
  waiting for transfers between devices  136 us (31%)
  other arithmetic  112 us (26%)
  blocking collectives  89.7 us (21%)
  starting transfers between devices  31.7 us (7%)
  local copies, waits for them, and re-layouts  25.9 us (6%)
  matrix products  23.6 us (5%)
  between operations  14.4 us (3%)
    another operation x10, other arithmetic, shards(): factor = jnp.linalg.cholesky(gram_matrix)  66.9 us
    psum x1, blocking collectives, shards(): lax.psum(transposed_product(matrix, sketch_cols), 'row')  59.9 us
    all_gather x1, waiting for transfers between devices, gather_axes(): value = lax.all_gather(value, axis, axis=dim, tiled=True)  53.4 us
    another operation x4, other arithmetic, shards(): jax.scipy.linalg.solve_triangular(factor, jnp.swapaxes(stacked, 1, 2), lo...  40.3 us
    all_to_all x1, waiting for transfers between devices, shards(): lax.all_to_all(outgoing, 'child', split_axis=0, concat_axis=0, tiled=True)  25.8 us
    all_to_all x1, waiting for transfers between devices, sum_at_owner_2(): tiles = lax.all_to_all(split_up(value, dim, peers), axis, 0, 0, tiled=True)  24.2 us
    all_to_all x1, waiting for transfers between devices, sent_to_all(): return lax.all_to_all(copies, axis, split_axis=0, concat_axis=0, tiled=True)  23.4 us
    all_to_all x1, blocking collectives, shards(): lax.all_to_all(back_buffer, 'child', split_axis=0, concat_axis=0, tiled=T...  19.2 us
  transfers between devices with their start and end apart: 5, of which 5 were waited for; matrix products, arithmetic and copies ran while one was open for 1% of the time, Pallas kernels for 0%

commit v1 on v0

v1 whole, which is shorter than its diff:
```python
import functools

import jax
import jax.numpy as jnp
from jax import lax
from jax.experimental import pallas as pl
from jax.experimental.pallas import tpu as pltpu
from jax.sharding import PartitionSpec as P

MESH = pl.DeviceIdType.MESH
F32, BF16 = jnp.float32, jnp.bfloat16
HIGHEST = lax.Precision.HIGHEST
VMEM_LIMIT = 60 * 1024 * 1024
SHIFT = 64.0


def ring(value, size):
    return lax.rem(value + 2 * size, size)


def dot(left, right, dims=((1,), (0,)), precision=None):
    return lax.dot_general(left, right, (dims, ((), ())), precision=precision, preferred_element_type=F32)


def greet(peers):
    barrier = pltpu.get_barrier_semaphore()
    for peer in peers:
        pl.semaphore_signal(barrier, inc=1, device_id=peer, device_id_type=MESH)
    pl.semaphore_wait(barrier, len(peers))


def send(source, target, send_sem, recv_sem, peer):
    copy = pltpu.make_async_remote_copy(
        src_ref=source,
        dst_ref=target,
        send_sem=send_sem,
        recv_sem=recv_sem,
        device_id=peer,
        device_id_type=MESH,
    )
    copy.start()
    return copy


def place():
    return lax.axis_index("child"), lax.axis_index("row"), lax.axis_index("col")


def columns(chunk):
    return pl.ds(pl.multiple_of(chunk * 256, 256), 256)


def hops_down(half):
    return 4 - half


def hops_up(half):
    return 3 + half


def sample_kernel(
    schur, sketch, block_map, own_out, gram_out,
    held, turned, part, sums_out, sums_in, power, total, b_out, b_in, c_out, c_in, z_all,
    load_sem, a_send, a_recv, p_send, p_recv, b_send, b_recv, c_send, c_recv, z_send, z_recv,
):
    c, r, k = place()
    pair, core = lax.div(c, 2), lax.rem(c, 2)
    below, above = {"row": ring(r - 1, 8)}, {"row": ring(r + 1, 8)}
    order = (4, 5, 3, 6, 2, 7, 1, 0)
    loads = {}
    for spot, rel in enumerate(order):
        chunk = ring(r + rel, 8)
        loads[rel] = pltpu.make_async_copy(schur.at[0, :, columns(chunk)], held.at[chunk], load_sem.at[spot])
        loads[rel].start()
    siblings = [{"child": ring(c + i, 8)} for i in range(1, 8)]
    group = [{"col": ring(k + i, 4)} for i in range(1, 4)]
    cross = [{"child": 2 * pair + 1 - core, "col": ring(k + i, 4)} for i in range(1, 4)]
    greet([below, above] + siblings + group + cross)
    turned[...] = sketch[...].T

    def produce(rel):
        chunk = ring(r + rel, 8)
        loads[rel].wait()
        part[chunk] = dot(turned[...], held[chunk])

    pending = []
    arriving = {}

    def pass_on(way, half, step):
        hops = hops_down(half) if way == 0 else hops_up(half)
        if step >= hops:
            return
        chunk = ring(r - hops + step if way == 0 else r + hops - step, 8)
        value = part[chunk, pl.ds(128 * half, 128)]
        if step:
            arriving[way, half, step - 1].wait_recv()
            value = value + sums_in[way, half, step - 1].astype(F32)
        sums_out[way, half, step] = value.astype(BF16)
        copy = send(
            sums_out.at[way, half, step], sums_in.at[way, half, step],
            a_send.at[way, half, step], a_recv.at[way, half, step], below if way == 0 else above,
        )
        arriving[way, half, step] = copy
        pending.append(copy)

    produce(4)
    pass_on(0, 0, 0)
    pass_on(1, 1, 0)
    produce(5)
    pass_on(0, 1, 0)
    produce(3)
    pass_on(1, 0, 0)
    for step, rels in ((1, (6, 2)), (2, (7, 1)), (3, (0,))):
        for rel in rels:
            produce(rel)
        for way, half in ((0, 0), (1, 1), (0, 1), (1, 0)):
            pass_on(way, half, step)
    for half in range(2):
        value = part[r, pl.ds(128 * half, 128)]
        for way, hops in ((0, hops_down(half)), (1, hops_up(half))):
            arriving[way, half, hops - 1].wait_recv()
            value = value + sums_in[way, half, hops - 1].astype(F32)
        power[r, pl.ds(128 * half, 128)] = value.astype(BF16)

    coming = {}

    def share(way, half, step):
        hops = 4 - half if way == 0 else 3 + half
        if step >= hops:
            return
        chunk = ring(r - step if way == 0 else r + step, 8)
        if step:
            coming[way, half, step - 1].wait_recv()
        ref = power.at[chunk, pl.ds(128 * half, 128)]
        copy = send(ref, ref, p_send.at[way, half, step], p_recv.at[way, half, step], above if way == 0 else below)
        coming[way, half, step] = copy
        pending.append(copy)

    def multiply(chunk):
        return dot(held[chunk], power[chunk], ((1,), (1,)))

    for step in range(4):
        for way in range(2):
            for half in range(2):
                share(way, half, step)
        if step == 0:
            total[...] = multiply(r)
            continue
        if step == 3:
            coming[0, 1, 2].wait_recv()
            coming[1, 0, 2].wait_recv()
        total[...] += multiply(ring(r - step, 8))
        total[...] += multiply(ring(r + step, 8))
    coming[0, 0, 3].wait_recv()
    coming[1, 1, 3].wait_recv()
    last = ring(r + 4, 8)
    copies = []
    for i in (2, 1, 3, 0):
        peer = ring(k + i, 4)
        rows = pl.ds(pl.multiple_of(peer * 256, 256), 256)
        value = total[rows] + dot(held[last, rows], power[last], ((1,), (1,)))
        if i:
            b_out[i - 1] = value.astype(BF16)
            copies.append(send(b_out.at[i - 1], b_in.at[i - 1], b_send.at[i - 1], b_recv.at[i - 1], {"col": peer}))
        else:
            summed = value
    for copy, i in zip(copies, (2, 1, 3)):
        copy.wait_recv()
        summed = summed + b_in[i - 1].astype(F32)
    pending += copies
    c_out[...] = summed.astype(BF16).reshape(2, 128, 256)

    copies = []
    for i in (4, 3, 5, 2, 6, 1, 7):
        peer = ring(c + i, 8)
        copies.append(send(c_out.at[lax.rem(peer, 2)], c_in.at[c], c_send.at[i - 1], c_recv.at[i - 1], {"child": peer}))
    c_in[c] = c_out[core]
    for copy in copies:
        copy.wait_recv()
    pending += copies
    spot = 8 * r + 2 * k + core
    value = jnp.zeros((128, 256), F32)
    for child in range(8):
        wanted = lax.shift_right_logical(block_map[child, spot], 3) == 4 * r + pair
        value = value + c_in[child].astype(F32) * jnp.where(wanted, 1.0, 0.0)
    own_out[...] = value
    offset = 2 * k + core
    z_all[offset] = value.astype(BF16)
    copies = []
    ref = z_all.at[offset]
    for i in (2, 1, 3, 0):
        peer = ring(k + i, 4)
        for other in range(2):
            if i == 0 and other == 0:
                continue
            slot = 2 * i + other - 1
            copies.append(send(ref, ref, z_send.at[slot], z_recv.at[slot],
                               {"child": c if other == 0 else 2 * pair + 1 - core, "col": peer}))
    for copy in copies:
        copy.wait_recv()
    pending += copies
    rows = z_all[...].reshape(1024, 256)
    gram_out[...] = dot(rows, rows, ((0,), (0,)))
    for copy in pending:
        copy.wait_send()


def coupling_kernel(
    schur, basis, block_map, owner_slot, basis_out, coupling_out,
    held, e_in, mine, column_in, row_in, total, sums, f_out, f_in, g_out, g_in, h_out, h_in,
    load_sem, e_send, e_recv, z_send, z_recv, y_send, y_recv, r_send, r_recv, f_send, f_recv, g_send, g_recv,
    h_send, h_recv,
):
    c, r, k = place()
    below, above = {"row": ring(r - 1, 8)}, {"row": ring(r + 1, 8)}
    loads = []
    for chunk in range(8):
        loads.append(pltpu.make_async_copy(schur.at[0, :, columns(chunk)], held.at[chunk], load_sem.at[chunk]))
        loads[-1].start()
    siblings = [{"child": ring(c + i, 8)} for i in range(1, 8)]
    greet([below, above] + siblings + [{"col": ring(k + i, 4)} for i in range(1, 4)])
    pending = []

    copies = []
    for i in (4, 3, 5, 2, 6, 1, 7):
        copies.append(send(basis, e_in.at[c], e_send.at[i - 1], e_recv.at[i - 1], {"child": ring(c + i, 8)}))
    e_in[c] = basis[...]
    for copy in copies:
        copy.wait_recv()
    pending += copies
    for half in range(2):
        near = lax.rem(lax.shift_right_logical(block_map[c, 8 * r + 2 * k + half], 3), 4)
        mine[r, pl.ds(128 * half, 128)] = e_in[2 * near + half]

    arriving = {}
    forwards = []

    def share(way, half, step):
        hops = 4 - half if way == 0 else 3 + half
        if step:
            arriving[way, half, step - 1].wait_recv()
        if step >= hops:
            return
        chunk = ring(r - step if way == 0 else r + step, 8)
        ref = mine.at[chunk, pl.ds(128 * half, 128)]
        copy = send(ref, ref, z_send.at[way, half, step], z_recv.at[way, half, step], above if way == 0 else below)
        arriving[way, half, step] = copy
        pending.append(copy)

    def across(rel, half):
        chunk = ring(r + rel, 8)
        peer = lax.div(chunk, 2)
        copy = pltpu.make_async_remote_copy(
            src_ref=mine.at[chunk, pl.ds(128 * half, 128)],
            dst_ref=column_in.at[lax.rem(chunk, 2), k, pl.ds(128 * half, 128)],
            send_sem=y_send.at[rel, half],
            recv_sem=y_recv.at[lax.rem(chunk, 2), k, half],
            device_id={"col": peer},
            device_id_type=MESH,
        )
        pl.when(peer != k)(copy.start)
        forwards.append((peer, copy))

    row_copies = []
    for half in range(2):
        share(0, half, 0)
        share(1, half, 0)
    for half in range(2):
        across(0, half)
    for i in (2, 1, 3):
        row_copies.append(send(mine.at[r], row_in.at[k], r_send.at[i - 1], r_recv.at[i - 1], {"col": ring(k + i, 4)}))
    row_in[k] = mine[r]

    for slot in range(2):
        for half in range(2):
            value = jnp.zeros((128, 256), F32)
            for g in range(4):
                wanted = owner_slot[4 * r + g] == 2 * c + slot
                value = value + e_in[2 * g + half].astype(F32) * jnp.where(wanted, 1.0, 0.0)
            basis_out[slot, 0, pl.ds(128 * half, 128)] = value

    for step in range(1, 5):
        for way, half in ((0, 0), (1, 1), (0, 1), (1, 0)):
            hops = 4 - half if way == 0 else 3 + half
            if step > hops:
                continue
            share(way, half, step)
            across((8 - step if way == 0 else step) % 8, half)
    for load in loads:
        load.wait()
    total[...] = dot(held[k], mine[2 * k]) + dot(held[4 + k], mine[2 * k + 1])
    for i in (1, 3, 2):
        peer = ring(k + i, 4)
        for odd in range(2):
            for half in range(2):
                pltpu.make_async_remote_copy(
                    src_ref=mine.at[0, pl.ds(128 * half, 128)],
                    dst_ref=column_in.at[odd, peer, pl.ds(128 * half, 128)],
                    send_sem=y_send.at[0, half],
                    recv_sem=y_recv.at[odd, peer, half],
                    device_id={"col": peer},
                    device_id_type=MESH,
                ).wait_recv()
            total[...] += dot(held[4 * odd + peer], column_in[odd, peer])
    for copy in row_copies:
        copy.wait_recv()
    pending += row_copies

    sums[...] = jnp.zeros_like(sums)
    for offset in range(8):
        value = total[pl.ds(128 * offset, 128)]
        high = value.astype(BF16)
        low = (value - high.astype(F32)).astype(BF16)
        left = row_in[offset // 2, pl.ds(128 * (offset % 2), 128)]
        product = dot(left, high, ((0,), (0,))) + dot(left, low, ((0,), (0,)))
        near = lax.rem(lax.shift_right_logical(block_map[c, 8 * r + offset], 3), 4)
        for g in range(4):
            sums[g] += product * jnp.where(near == g, 1.0, 0.0)

    copies = []
    for i in (2, 1, 3):
        peer = ring(k + i, 4)
        rows = pl.ds(pl.multiple_of(peer * 64, 64), 64)
        f_out[i - 1] = sums[:, rows].astype(BF16)
        copies.append(send(f_out.at[i - 1], f_in.at[i - 1], f_send.at[i - 1], f_recv.at[i - 1], {"col": peer}))
    value = sums[:, pl.ds(pl.multiple_of(k * 64, 64), 64)]
    for copy, i in zip(copies, (2, 1, 3)):
        copy.wait_recv()
        value = value + f_in[i - 1].astype(F32)
    pending += copies
    g_out[...] = value.astype(BF16).reshape(8, 32, 256)
    copies = []
    for i in (4, 3, 5, 2, 6, 1, 7):
        peer = ring(c + i, 8)
        copies.append(send(g_out.at[peer], g_in.at[c], g_send.at[i - 1], g_recv.at[i - 1], {"child": peer}))
    g_in[c] = g_out[c]
    for copy in copies:
        copy.wait_recv()
    pending += copies
    h_out[...] = jnp.sum(g_in[...].astype(F32), axis=0).astype(BF16)
    copies = []
    for i in (4, 3, 5, 2, 6, 1, 7):
        copies.append(send(h_out, h_in.at[c], h_send.at[i - 1], h_recv.at[i - 1], {"child": ring(c + i, 8)}))
    h_in[c] = h_out[...]
    for copy in copies:
        copy.wait_recv()
    pending += copies
    for slot in range(2):
        for half in range(2):
            value = jnp.zeros((32, 256), F32)
            for g in range(4):
                wanted = owner_slot[4 * r + g] == 2 * c + slot
                value = value + h_in[2 * g + half].astype(F32) * jnp.where(wanted, 1.0, 0.0)
            coupling_out[slot, 0, pl.ds(32 * half, 32)] = value
    for copy in pending:
        copy.wait_send()
    for peer, copy in forwards:
        pl.when(peer != k)(copy.wait_send)


def orthonormal(own, gram):
    factor = jnp.linalg.cholesky(gram + SHIFT * jnp.eye(256, dtype=F32))
    return jax.scipy.linalg.solve_triangular(factor, own.T, lower=True).T


def in_vmem():
    return pl.BlockSpec(memory_space=pltpu.VMEM)


def in_smem():
    return pl.BlockSpec(memory_space=pltpu.SMEM)


def sampled(schur, sketch, block_map):
    dma = pltpu.SemaphoreType.DMA
    return pl.pallas_call(
        sample_kernel,
        out_shape=(jax.ShapeDtypeStruct((128, 256), F32), jax.ShapeDtypeStruct((256, 256), F32)),
        in_specs=[pl.BlockSpec(memory_space=pl.ANY), in_vmem(), in_smem()],
        out_specs=(in_vmem(), in_vmem()),
        scratch_shapes=[
            pltpu.VMEM((8, 1024, 256), BF16),
            pltpu.VMEM((256, 1024), BF16),
            pltpu.VMEM((8, 256, 256), F32),
            pltpu.VMEM((2, 2, 4, 128, 256), BF16),
            pltpu.VMEM((2, 2, 4, 128, 256), BF16),
            pltpu.VMEM((8, 256, 256), BF16),
            pltpu.VMEM((1024, 256), F32),
            pltpu.VMEM((3, 256, 256), BF16),
            pltpu.VMEM((3, 256, 256), BF16),
            pltpu.VMEM((2, 128, 256), BF16),
            pltpu.VMEM((8, 128, 256), BF16),
            pltpu.VMEM((8, 128, 256), BF16),
            dma((8,)),
            dma((2, 2, 4)), dma((2, 2, 4)),
            dma((2, 2, 4)), dma((2, 2, 4)),
            dma((3,)), dma((3,)),
            dma((7,)), dma((7,)),
            dma((8,)), dma((8,)),
        ],
        compiler_params=pltpu.CompilerParams(
            collective_id=0, has_side_effects=True, vmem_limit_bytes=VMEM_LIMIT
        ),
        name="samples",
    )(schur, sketch, block_map)


def coupled(schur, basis, block_map, owner_slot):
    dma = pltpu.SemaphoreType.DMA
    return pl.pallas_call(
        coupling_kernel,
        out_shape=(
            jax.ShapeDtypeStruct((2, 1, 256, 256), F32),
            jax.ShapeDtypeStruct((2, 1, 64, 256), F32),
        ),
        in_specs=[pl.BlockSpec(memory_space=pl.ANY), in_vmem(), in_smem(), in_smem()],
        out_specs=(in_vmem(), in_vmem()),
        scratch_shapes=[
            pltpu.VMEM((8, 1024, 256), BF16),
            pltpu.VMEM((8, 128, 256), BF16),
            pltpu.VMEM((8, 256, 256), BF16),
            pltpu.VMEM((2, 4, 256, 256), BF16),
            pltpu.VMEM((4, 256, 256), BF16),
            pltpu.VMEM((1024, 256), F32),
            pltpu.VMEM((4, 256, 256), F32),
            pltpu.VMEM((3, 4, 64, 256), BF16),
            pltpu.VMEM((3, 4, 64, 256), BF16),
            pltpu.VMEM((8, 32, 256), BF16),
            pltpu.VMEM((8, 32, 256), BF16),
            pltpu.VMEM((32, 256), BF16),
            pltpu.VMEM((8, 32, 256), BF16),
            dma((8,)),
            dma((7,)), dma((7,)),
            dma((2, 2, 4)), dma((2, 2, 4)),
            dma((8, 2)), dma((2, 4, 2)),
            dma((3,)), dma((3,)),
            dma((3,)), dma((3,)),
            dma((7,)), dma((7,)),
            dma((7,)), dma((7,)),
        ],
        compiler_params=pltpu.CompilerParams(
            collective_id=1, has_side_effects=True, vmem_limit_bytes=VMEM_LIMIT
        ),
        name="coupling",
    )(schur, basis, block_map, owner_slot)


def shards(schur_blocks, sketch_cols, block_map, owner_slot):
    own, gram = sampled(schur_blocks, sketch_cols, block_map)
    basis = orthonormal(own, gram)
    return coupled(schur_blocks, basis.astype(BF16), block_map, owner_slot)


def solution(mesh):
    placed = (P("child", "row", "col"), P("row", None), P(), P())
    return jax.shard_map(
        shards,
        mesh=mesh,
        in_specs=placed,
        out_specs=(P("child", "row", "col", None), P("child", "row", "col", None)),
        check_vma=False,
    )
```

time: 434 us -> 189 us (0.44)
  waiting for transfers between devices: 136 us -> 0 us
  Pallas kernels: 0 us -> 121 us
  blocking collectives: 89.7 us -> 0 us
  other arithmetic: 112 us -> 54.6 us
  starting transfers between devices: 31.7 us -> 0 us
  matrix products: 23.6 us -> 1.25 us
  local copies, waits for them, and re-layouts: 25.9 us -> 9.43 us
  between operations: 14.4 us -> 2.17 us
    pallas_call x0 -> x2, Pallas kernels: none -> 121 us  [the longest x1 66.1 us: sampled(): pl.pallas_call(sample_kernel, out_shape=(jax.ShapeDtypeStruct((128, 256),...]
    all_to_all x4 -> x0, waiting for transfers between devices: 82.3 us -> none  [the longest x1 25.8 us: shards(): lax.all_to_all(outgoing, 'child', split_axis=0, concat_axis=0, tiled=True)]
    psum x1 -> x0, blocking collectives: 59.9 us -> none  [shards(): lax.psum(transposed_product(matrix, sketch_cols), 'row')]
    another operation x15 -> x9, other arithmetic: 107 us -> 53.9 us  [the longest x6 34.2 us: orthonormal(): factor = jnp.linalg.cholesky(gram + SHIFT * jnp.eye(256, dtype=F32))]
    all_gather x1 -> x0, waiting for transfers between devices: 53.4 us -> none  [gather_axes(): value = lax.all_gather(value, axis, axis=dim, tiled=True)]
    all_to_all x4 -> x0, starting transfers between devices: 31.5 us -> none  [the longest x1 16 us: shards(): lax.all_to_all(outgoing, 'child', split_axis=0, concat_axis=0, tiled=True)]
    dot_general x11 -> x0, matrix products: 21.7 us -> none  [the longest x1 4.8 us: shards(): jnp.dot(matrix, column_basis, preferred_element_type=jnp.float32)]
    all_to_all x1 -> x0, blocking collectives: 19.2 us -> none  [shards(): lax.all_to_all(back_buffer, 'child', split_axis=0, concat_axis=0, tiled=T...]
  transfers between devices with their start and end apart: 5 -> 0, of which waited for: 5 -> 0; matrix products, arithmetic and copies ran while one was open for 1% -> 0% of each run, Pallas kernels for 0% -> 0%
where the time goes in v1:
time: 189 us
  Pallas kernels  121 us (64%)
  other arithmetic  54.6 us (29%)
  local copies, waits for them, and re-layouts  9.43 us (5%)
  between operations  2.17 us (1%)
    pallas_call x1, Pallas kernels, sampled(): pl.pallas_call(sample_kernel, out_shape=(jax.ShapeDtypeStruct((128, 256),...  66.1 us
    pallas_call x1, Pallas kernels, coupled(): pl.pallas_call(coupling_kernel, out_shape=(jax.ShapeDtypeStruct((2, 1, 25...  55.1 us
    another operation x6, other arithmetic, orthonormal(): factor = jnp.linalg.cholesky(gram + SHIFT * jnp.eye(256, dtype=F32))  34.2 us
    another operation x3, other arithmetic, orthonormal(): return jax.scipy.linalg.solve_triangular(factor, own.T, lower=True).T  19.7 us
    another operation x10, local copies, waits for them, and re-layouts  4.26 us

profile of v1, /device:TPU:1, one launch (start us, length us, event | category | flops | bytes accessed | tf_op | source)
XLA Modules:
  0.0 188.7 jit_solution(13032881272779523089)
XLA Ops:
  0.6 0.1 triangular_solve.60
  0.7 66.1 %samples.1 = (f32[128,256]{1,0:T(8,128)}, f32[256,256]{1,0:T(8,128)}) custom-call(bf16[1,1024,2048]{2,1,0:T(8,128)(2,1)} %schur.3, bf16[1024,256]{1,0:T(8,128)(2,1)} %sketch.1, s32[8,64]{1,0:T(8,128)} %block_map.3), custom_call_target="tpu_custom_call" | custom-call | tf_op jit(solution)/shard_map/samples/pallas_call | solution.py:376
  66.8 0.0 copy-start
  66.8 1.1 copy.6
  68.0 0.1 copy.7
  68.2 11.7 %cholesky.49 = f32[128,128]{1,0:T(8,128)S(1)} custom-call(f32[128,128]{1,0:T(8,128)S(1)} %cholesky.115), custom_call_target="Cholesky" | custom-call | tf_op jit(solution)/shard_map/jit(cholesky)/cholesky | solution.py:362
  79.9 0.1 copy.8
  80.0 9.8 %custom-call.15 = f32[1,128,128]{1,2,0:T(8,128)S(1)} custom-call(f32[1,128,128]{2,1,0:T(8,128)S(1)} %get-tuple-element.29), custom_call_target="InvertDiagBlocksLowerTriangular" | custom-call | tf_op jit(solution)/shard_map/jit(cholesky)/cholesky | solution.py:362
  89.8 0.2 fusion.4
  90.0 0.3 convolution_subtract_fusion.1
  90.3 11.9 %cholesky.103 = f32[128,128]{1,0:T(8,128)S(1)} custom-call(f32[128,128]{1,0:T(8,128)S(1)} %convolution_subtract_fusion.1), custom_call_target="Cholesky" | custom-call | tf_op jit(solution)/shard_map/jit(cholesky)/cholesky | solution.py:362
  102.2 0.1 copy.9
  102.3 0.1 copy.10
  102.4 0.7 compare_reduce_fusion
  104.6 4.3 %while.1 = (s32[]{:T(128)}, f32[256,256]{0,1:T(8,128)S(1)}, s32[2,2]{1,0:T(2,128)S(1)}, f32[2,128,128]{2,1,0:T(8,128)S(1)}, s32[]{:T(128)}) while((s32[]{:T(128)}, f32[256,256]{0,1:T(8,128)S(1)}, s32[2,2]{1,0:T(2,128)S(1)}, f32[2,128,128]{2,1,0:T(8,128)S(1)}, s32[]{:T(128)}) %tuple.24), condition=%wide.while_cond, body=%wide.while_body.sunk | while | flops 2 | bytes 393329 | solution.py:363
  104.6 0.6 fusion.13
  105.2 1.4 dynamic-slice.7
  106.6 0.1 copy.17
  106.8 0.6 fusion.13
  107.4 1.4 dynamic-slice.7
  108.8 0.1 copy.17
  108.9 19.7 %custom-call.16 = f32[2,128,128]{1,2,0:T(8,128)S(1)} custom-call(f32[2,128,128]{2,1,0:T(8,128)S(1)} %get-tuple-element.13), custom_call_target="InvertDiagBlocksLowerTriangular" | custom-call | tf_op jit(solution)/shard_map/jit(_solve_triangular)/triangular_solve | solution.py:363
  128.6 0.0 copy-done
  128.6 0.3 fusion.2
  128.9 0.3 convolution_subtract_fusion
  129.2 0.2 convolution_convert_fusion
  129.4 0.1 copy.12
  129.5 0.6 maximum_bitcast_fusion.basis
  130.2 55.1 %coupling.1 = (f32[2,1,256,256]{3,2,1,0:T(8,128)}, f32[2,1,64,256]{3,2,1,0:T(8,128)}) custom-call(bf16[1,1024,2048]{2,1,0:T(8,128)(2,1)} %schur.3, bf16[128,256]{1,0:T(8,128)(2,1)} %maximum_bitcast_fusion.basis, s32[8,64]{1,0:T(8,128)} %block_map.3, s32[32]{0:T(128)} %owner_slot.1), custom_call_target="tpu_custom_call" | custom-call | tf_op jit(solution)/shard_map/coupling/pallas_call | solution.py:410
  185.3 1.9 copy.31
  187.1 1.6 copy.32
  (15 shorter events, 0.3 us)
Async XLA Ops:
  66.8 61.8 %copy-start = (f32[128,256]{1,0:T(8,128)S(1)}, f32[128,256]{1,0:T(8,128)}, u32[]{:S(2)}) copy-start(f32[128,256]{1,0:T(8,128)} %get-tuple-element.5) | copy-start | bytes 393220

commit v2 on v1

--- a/solution.py
+++ b/solution.py
@@ -358,13 +358,95 @@
         pl.when(peer != k)(copy.wait_send)
 
 
-def orthonormal(own, gram):
-    factor = jnp.linalg.cholesky(gram + SHIFT * jnp.eye(256, dtype=F32))
-    return jax.scipy.linalg.solve_triangular(factor, own.T, lower=True).T
+def lanes(value, column):
+    return jnp.broadcast_to(value[:, column : column + 1], (8, 128))
+
+
+def sublanes(value, row):
+    return jnp.broadcast_to(value[row : row + 1, :], (8, 128))
+
+
+def inverse_factor(rows, marks):
+    sub = lax.broadcasted_iota(jnp.int32, (8, 128), 0)
+    for i in range(16):
+        left = [[lanes(rows[t], 8 * i + p) for p in range(8)] for t in range(i, 16)]
+        inner = {(q, p): sublanes(left[0][p], q) for p in range(8) for q in range(p, 8)}
+        upper = [sublanes(rows[i], p) for p in range(8)]
+        done = [sublanes(marks[i], p) for p in range(8)]
+        for p in range(8):
+            scale = lax.rsqrt(inner[p, p])
+            for q in range(p + 1, 8):
+                inner[q, p] = inner[q, p] * scale
+            upper[p] = upper[p] * scale
+            done[p] = done[p] * scale
+            for t in range(1, 16 - i):
+                left[t][p] = left[t][p] * scale
+            for q in range(p + 1, 8):
+                for s in range(q, 8):
+                    inner[s, q] = inner[s, q] - inner[s, p] * inner[q, p]
+                upper[q] = upper[q] - inner[q, p] * upper[p]
+                done[q] = done[q] - inner[q, p] * done[p]
+                for t in range(1, 16 - i):
+                    left[t][q] = left[t][q] - left[t][p] * inner[q, p]
+        for t in range(1, 16 - i):
+            for p in range(8):
+                if i + 1 < 16:
+                    rows[i + t] = rows[i + t] - left[t][p] * upper[p]
+                marks[i + t] = marks[i + t] - left[t][p] * done[p]
+        value = done[0]
+        for p in range(1, 8):
+            value = jnp.where(sub == p, done[p], value)
+        marks[i] = value
+    return marks
+
+
+def basis_kernel(own, gram, out, work, inverse, below):
+    row = lax.broadcasted_iota(jnp.int32, (128, 128), 0)
+    column = lax.broadcasted_iota(jnp.int32, (128, 128), 1)
+    work[...] = gram[:128, :128] + jnp.where(row == column, SHIFT, 0.0)
+
+    def step(part, carry):
+        rows = [work[pl.ds(8 * t, 8)] for t in range(16)]
+        sub = lax.broadcasted_iota(jnp.int32, (8, 128), 0)
+        lane = lax.broadcasted_iota(jnp.int32, (8, 128), 1)
+        marks = [jnp.where(lane == sub + 8 * t, 1.0, 0.0) for t in range(16)]
+        marks = inverse_factor(rows, marks)
+        for t in range(16):
+            inverse[part, pl.ds(8 * t, 8)] = marks[t]
+
+        @pl.when(part == 0)
+        def _():
+            below[...] = dot(gram[128:, :128], inverse[0], ((1,), (1,)), HIGHEST)
+            work[...] = (
+                gram[128:, 128:] + jnp.where(row == column, SHIFT, 0.0)
+                - dot(below[...], below[...], ((1,), (1,)), HIGHEST)
+            )
+        return carry
+
+    lax.fori_loop(0, 2, step, 0)
+    first = dot(own[:, :128], inverse[0], ((1,), (1,)), HIGHEST)
+    out[:, :128] = first.astype(BF16)
+    rest = own[:, 128:] - dot(first, below[...], ((1,), (1,)), HIGHEST)
+    out[:, 128:] = dot(rest, inverse[1], ((1,), (1,)), HIGHEST).astype(BF16)
 
 
 def in_vmem():
     return pl.BlockSpec(memory_space=pltpu.VMEM)
+
+
+def orthonormal(own, gram):
+    return pl.pallas_call(
+        basis_kernel,
+        out_shape=jax.ShapeDtypeStruct((128, 256), BF16),
+        in_specs=[in_vmem(), in_vmem()],
+        out_specs=in_vmem(),
+        scratch_shapes=[
+            pltpu.VMEM((128, 128), F32),
+            pltpu.VMEM((2, 128, 128), F32),
+            pltpu.VMEM((128, 128), F32),
+        ],
+        name="basis",
+    )(own, gram)
 
 
 def in_smem():
@@ -448,7 +530,7 @@
 def shards(schur_blocks, sketch_cols, block_map, owner_slot):
     own, gram = sampled(schur_blocks, sketch_cols, block_map)
     basis = orthonormal(own, gram)
-    return coupled(schur_blocks, basis.astype(BF16), block_map, owner_slot)
+    return coupled(schur_blocks, basis, block_map, owner_slot)
 
 
 def solution(mesh):

time: 189 us -> 138 us (0.73)
  other arithmetic: 54.6 us -> 0 us
  Pallas kernels: 121 us -> 134 us
  local copies, waits for them, and re-layouts: 9.43 us -> 3.44 us
    another operation x9 -> x0, other arithmetic: 53.9 us -> none  [the longest x6 34.2 us: orthonormal(): factor = jnp.linalg.cholesky(gram + SHIFT * jnp.eye(256, dtype=F32))]
    pallas_call x0 -> x1, Pallas kernels: none -> 12.6 us  [orthonormal(): pl.pallas_call(basis_kernel, out_shape=jax.ShapeDtypeStruct((128, 256), B...]
    another operation x19 -> x0, local copies, waits for them, and re-layouts: 4.75 us -> none
where the time goes in v2:
time: 138 us
  Pallas kernels  134 us (97%)
  local copies, waits for them, and re-layouts  3.44 us (2%)
    pallas_call x1, Pallas kernels, sampled(): pl.pallas_call(sample_kernel, out_shape=(jax.ShapeDtypeStruct((128, 256),...  66.1 us
    pallas_call x1, Pallas kernels, coupled(): pl.pallas_call(coupling_kernel, out_shape=(jax.ShapeDtypeStruct((2, 1, 25...  55 us
    pallas_call x1, Pallas kernels, orthonormal(): pl.pallas_call(basis_kernel, out_shape=jax.ShapeDtypeStruct((128, 256), B...  12.6 us
    unnamed x2, local copies, waits for them, and re-layouts  3.44 us

profile of v2, /device:TPU:1, one launch (start us, length us, event | category | flops | bytes accessed | tf_op | source)
XLA Modules:
  0.0 137.8 jit_solution(5377064718701537522)
XLA Ops:
  0.6 66.1 %samples.1 = (f32[128,256]{1,0:T(8,128)}, f32[256,256]{1,0:T(8,128)}) custom-call(bf16[1,1024,2048]{2,1,0:T(8,128)(2,1)} %schur.3, bf16[1024,256]{1,0:T(8,128)(2,1)} %sketch.1, s32[8,64]{1,0:T(8,128)} %block_map.3), custom_call_target="tpu_custom_call" | custom-call | tf_op jit(solution)/shard_map/samples/pallas_call | solution.py:458
  66.8 12.6 %basis.1 = bf16[128,256]{1,0:T(8,128)(2,1)} custom-call(f32[128,256]{1,0:T(8,128)} %get-tuple-element.4.own, f32[256,256]{1,0:T(8,128)} %get-tuple-element.5.gram), custom_call_target="tpu_custom_call" | custom-call | tf_op jit(solution)/shard_map/basis/pallas_call | solution.py:438
  79.3 55.0 %coupling.1 = (f32[2,1,256,256]{3,2,1,0:T(8,128)}, f32[2,1,64,256]{3,2,1,0:T(8,128)}) custom-call(bf16[1,1024,2048]{2,1,0:T(8,128)(2,1)} %schur.3, bf16[128,256]{1,0:T(8,128)(2,1)} %basis.1, s32[8,64]{1,0:T(8,128)} %block_map.3, s32[32]{0:T(128)} %owner_slot.1), custom_call_target="tpu_custom_call" | custom-call | tf_op jit(solution)/shard_map/coupling/pallas_call | solution.py:492
  134.3 1.9 %copy.8 = f32[2,1,256,256]{3,2,1,0:T(8,128)} copy(f32[2,1,256,256]{3,2,1,0:T(8,128)} %get-tuple-element.8) | data formatting | bytes 1048576
  136.2 1.6 %copy.9 = f32[2,1,64,256]{3,2,1,0:T(8,128)} copy(f32[2,1,64,256]{3,2,1,0:T(8,128)} %get-tuple-element.9) | data formatting | bytes 262144

commit v3 on v1

v3 whole, which is shorter than its diff:
```python
import functools

import jax
import jax.numpy as jnp
from jax import lax
from jax.experimental import pallas as pl
from jax.experimental.pallas import tpu as pltpu
from jax.sharding import PartitionSpec as P

MESH = pl.DeviceIdType.MESH
F32, BF16 = jnp.float32, jnp.bfloat16
HIGHEST = lax.Precision.HIGHEST
VMEM_LIMIT = 60 * 1024 * 1024
SHIFT = 64.0


def ring(value, size):
    return lax.rem(value + 2 * size, size)


def dot(left, right, dims=((1,), (0,)), precision=None):
    return lax.dot_general(left, right, (dims, ((), ())), precision=precision, preferred_element_type=F32)


def hello(peers):
    for peer in peers:
        pl.semaphore_signal(pltpu.get_barrier_semaphore(), inc=1, device_id=peer, device_id_type=MESH)


def met(peers):
    pl.semaphore_wait(pltpu.get_barrier_semaphore(), len(peers))


def send(source, target, send_sem, recv_sem, peer):
    copy = pltpu.make_async_remote_copy(
        src_ref=source,
        dst_ref=target,
        send_sem=send_sem,
        recv_sem=recv_sem,
        device_id=peer,
        device_id_type=MESH,
    )
    copy.start()
    return copy


def place():
    return lax.axis_index("child"), lax.axis_index("row"), lax.axis_index("col")


def columns(chunk):
    return pl.ds(pl.multiple_of(chunk * 256, 256), 256)


def lanes(value, column):
    return jnp.broadcast_to(value[:, column : column + 1], (8, 128))


def sublanes(value, row):
    return jnp.broadcast_to(value[row : row + 1, :], (8, 128))


def inverse_factor(rows, marks):
    sub = lax.broadcasted_iota(jnp.int32, (8, 128), 0)
    for i in range(16):
        left = [[lanes(rows[t], 8 * i + p) for p in range(8)] for t in range(i, 16)]
        inner = {(q, p): sublanes(left[0][p], q) for p in range(8) for q in range(p, 8)}
        upper = [sublanes(rows[i], p) for p in range(8)]
        done = [sublanes(marks[i], p) for p in range(8)]
        for p in range(8):
            scale = lax.rsqrt(inner[p, p])
            for q in range(p + 1, 8):
                inner[q, p] = inner[q, p] * scale
            upper[p] = upper[p] * scale
            done[p] = done[p] * scale
            for t in range(1, 16 - i):
                left[t][p] = left[t][p] * scale
            for q in range(p + 1, 8):
                for s in range(q, 8):
                    inner[s, q] = inner[s, q] - inner[s, p] * inner[q, p]
                upper[q] = upper[q] - inner[q, p] * upper[p]
                done[q] = done[q] - inner[q, p] * done[p]
                for t in range(1, 16 - i):
                    left[t][q] = left[t][q] - left[t][p] * inner[q, p]
        for t in range(1, 16 - i):
            for p in range(8):
                if i + 1 < 16:
                    rows[i + t] = rows[i + t] - left[t][p] * upper[p]
                marks[i + t] = marks[i + t] - left[t][p] * done[p]
        value = done[0]
        for p in range(1, 8):
            value = jnp.where(sub == p, done[p], value)
        marks[i] = value
        yield i


def row_blocks(value):
    return [value[8 * t : 8 * t + 8] for t in range(16)]


def identity(scale):
    row = lax.broadcasted_iota(jnp.int32, (128, 128), 0)
    column = lax.broadcasted_iota(jnp.int32, (128, 128), 1)
    return jnp.where(row == column, scale, 0.0)


def sample_kernel(
    schur, sketch, block_map, own_out, gram_out,
    held, turned, part, sums_out, sums_in, power, total, b_out, b_in, c_out, c_in, z_all,
    load_sem, a_send, a_recv, p_send, p_recv, b_send, b_recv, c_send, c_recv, z_send, z_recv,
):
    c, r, k = place()
    pair, core = lax.div(c, 2), lax.rem(c, 2)
    below, above = {"row": ring(r - 1, 8)}, {"row": ring(r + 1, 8)}
    siblings = [{"child": ring(c + i, 8)} for i in range(1, 8)]
    group = [{"col": ring(k + i, 4)} for i in range(1, 4)]
    cross = [{"child": 2 * pair + 1 - core, "col": ring(k + i, 4)} for i in range(1, 4)]
    peers = [below, above] + siblings + group + cross
    hello(peers)
    loads = {}
    for spot, rel in enumerate((4, 5, 3, 6, 2, 7, 1, 0)):
        chunk = ring(r + rel, 8)
        loads[rel] = pltpu.make_async_copy(schur.at[0, :, columns(chunk)], held.at[chunk], load_sem.at[spot])
        loads[rel].start()
    turned[...] = sketch[...].T

    def produce(rel):
        chunk = ring(r + rel, 8)
        loads[rel].wait()
        part[chunk] = dot(turned[...], held[chunk])

    pending = []
    arriving = {}
    lanesets = ((0, 0), (1, 1), (0, 1), (1, 0))

    def pass_on(s, way, u, step):
        hops = 4 - u if way == 0 else 3 + u
        if step >= hops:
            return
        chunk = ring(r - hops + step if way == 0 else r + hops - step, 8)
        value = part[chunk, pl.ds(128 * s + 64 * u, 64)]
        if step:
            arriving[s, way, u, step - 1].wait_recv()
            value = value + sums_in[s, way, u, step - 1].astype(F32)
        sums_out[s, way, u, step] = value.astype(BF16)
        copy = send(
            sums_out.at[s, way, u, step], sums_in.at[s, way, u, step],
            a_send.at[s, way, u, step], a_recv.at[s, way, u, step], below if way == 0 else above,
        )
        arriving[s, way, u, step] = copy
        pending.append(copy)

    produce(4)
    met(peers)
    for s in range(2):
        pass_on(s, 0, 0, 0)
        pass_on(s, 1, 1, 0)
    produce(5)
    for s in range(2):
        pass_on(s, 0, 1, 0)
    produce(3)
    for s in range(2):
        pass_on(s, 1, 0, 0)
    for step, rels in ((1, (6, 2)), (2, (7, 1)), (3, (0,))):
        for rel in rels:
            produce(rel)
        for s in range(2):
            for way, u in lanesets:
                pass_on(s, way, u, step)

    def finish_sum(s):
        for u in range(2):
            value = part[r, pl.ds(128 * s + 64 * u, 64)]
            for way, hops in ((0, 4 - u), (1, 3 + u)):
                arriving[s, way, u, hops - 1].wait_recv()
                value = value + sums_in[s, way, u, hops - 1].astype(F32)
            power[s, r, pl.ds(64 * u, 64)] = value.astype(BF16)

    coming = {}

    def share(s, way, u, step):
        hops = 4 - u if way == 0 else 3 + u
        if step and step <= hops:
            coming[s, way, u, step - 1].wait_recv()
        if step >= hops:
            return
        chunk = ring(r - step if way == 0 else r + step, 8)
        ref = power.at[s, chunk, pl.ds(64 * u, 64)]
        copy = send(
            ref, ref, p_send.at[s, way, u, step], p_recv.at[s, way, u, step], above if way == 0 else below
        )
        coming[s, way, u, step] = copy
        pending.append(copy)

    def multiply(s, chunk):
        return dot(held[chunk], power[s, chunk], ((1,), (1,)))

    for s in range(2):
        finish_sum(s)
        for way, u in lanesets:
            share(s, way, u, 0)
    for s in range(2):
        total[s] = multiply(s, r)
    for step in range(1, 4):
        for s in range(2):
            for way, u in lanesets:
                share(s, way, u, step)
            total[s] += multiply(s, ring(r - step, 8)) + multiply(s, ring(r + step, 8))

    last = ring(r + 4, 8)
    summed, sent = {}, {}
    for s in range(2):
        share(s, 0, 0, 4)
        share(s, 1, 1, 4)
        sent[s] = []
        for i in (2, 1, 3, 0):
            peer = ring(k + i, 4)
            rows = pl.ds(pl.multiple_of(peer * 256, 256), 256)
            value = total[s, rows] + dot(held[last, rows], power[s, last], ((1,), (1,)))
            if i:
                b_out[s, i - 1] = value.astype(BF16)
                copy = send(
                    b_out.at[s, i - 1], b_in.at[s, i - 1], b_send.at[s, i - 1], b_recv.at[s, i - 1], {"col": peer}
                )
                sent[s].append((i, copy))
                pending.append(copy)
            else:
                total[s, rows] = value

    swapped = {}
    for s in range(2):
        value = total[s, pl.ds(pl.multiple_of(k * 256, 256), 256)]
        for i, copy in sent[s]:
            copy.wait_recv()
            value = value + b_in[s, i - 1].astype(F32)
        c_out[s] = value.astype(BF16).reshape(2, 128, 128)
        swapped[s] = []
        for i in (4, 3, 5, 2, 6, 1, 7):
            peer = ring(c + i, 8)
            copy = send(
                c_out.at[s, lax.rem(peer, 2)], c_in.at[s, c], c_send.at[s, i - 1], c_recv.at[s, i - 1], {"child": peer}
            )
            swapped[s].append(copy)
            pending.append(copy)
        c_in[s, c] = c_out[s, core]

    spot = 8 * r + 2 * k + core
    offset = 2 * k + core
    gathered = {}
    for s in range(2):
        for copy in swapped[s]:
            copy.wait_recv()
        value = jnp.zeros((128, 128), F32)
        for child in range(8):
            wanted = lax.shift_right_logical(block_map[child, spot], 3) == 4 * r + pair
            value = value + c_in[s, child].astype(F32) * jnp.where(wanted, 1.0, 0.0)
        own_out[:, pl.ds(128 * s, 128)] = value
        z_all[s, offset] = value.astype(BF16)
        gathered[s] = []
        ref = z_all.at[s, offset]
        for i in (2, 1, 3, 0):
            for other in range(2):
                if i == 0 and other == 0:
                    continue
                slot = 2 * i + other
                copy = send(
                    ref, ref, z_send.at[s, slot], z_recv.at[s, slot],
                    {"child": c if other == 0 else 2 * pair + 1 - core, "col": ring(k + i, 4)},
                )
                gathered[s].append(copy)
                pending.append(copy)
    for copy in gathered[0]:
        copy.wait_recv()
    first = z_all[0].reshape(1024, 128)
    gram_out[0] = dot(first, first, ((0,), (0,)))
    for copy in gathered[1]:
        copy.wait_recv()
    second = z_all[1].reshape(1024, 128)
    gram_out[1] = dot(second, first, ((0,), (0,)))
    gram_out[2] = dot(second, second, ((0,), (0,)))
    for copy in pending:
        copy.wait_send()


def coupling_kernel(
    schur, own, gram, block_map, owner_slot, basis_out, coupling_out,
    held, inverse, corner, front, b_own, e_low, e_high, mine, column_in, row_in, total, sums,
    f_out, f_in, g_out, g_in, h_out, h_in,
    load_sem, e_send, e_recv, z_send, z_recv, y_send, y_recv, r_send, r_recv, f_send, f_recv, g_send, g_recv,
    h_send, h_recv,
):
    c, r, k = place()
    below, above = {"row": ring(r - 1, 8)}, {"row": ring(r + 1, 8)}
    siblings = [{"child": ring(c + i, 8)} for i in range(1, 8)]
    peers = [below, above] + siblings + [{"col": ring(k + i, 4)} for i in range(1, 4)]
    hello(peers)
    loads = []
    for chunk in range(8):
        loads.append(pltpu.make_async_copy(schur.at[0, :, columns(chunk)], held.at[chunk], load_sem.at[chunk]))
        loads[-1].start()
    pending = []
    outgoing = {}
    e_in = (e_low, e_high)

    def spread(s):
        outgoing[s] = []
        for i in (4, 3, 5, 2, 6, 1, 7):
            copy = send(
                b_own.at[s], e_in[s].at[c], e_send.at[s, i - 1], e_recv.at[s, i - 1], {"child": ring(c + i, 8)}
            )
            outgoing[s].append(copy)
            pending.append(copy)
        e_in[s][c] = b_own[s]

    def select(s):
        for copy in outgoing[s]:
            copy.wait_recv()
        for half in range(2):
            near = lax.rem(lax.shift_right_logical(block_map[c, 8 * r + 2 * k + half], 3), 4)
            mine[s, r, pl.ds(128 * half, 128)] = e_in[s][2 * near + half]

    arriving = {}
    forwards = []
    lanesets = ((0, 0), (1, 1), (0, 1), (1, 0))

    def across(s, rel, half):
        chunk = ring(r + rel, 8)
        peer = lax.div(chunk, 2)
        copy = pltpu.make_async_remote_copy(
            src_ref=mine.at[s, chunk, pl.ds(128 * half, 128)],
            dst_ref=column_in.at[s, lax.rem(chunk, 2), k, pl.ds(128 * half, 128)],
            send_sem=y_send.at[s, rel, half],
            recv_sem=y_recv.at[s, lax.rem(chunk, 2), k, half],
            device_id={"col": peer},
            device_id_type=MESH,
        )
        pl.when(peer != k)(copy.start)
        forwards.append((peer, copy))

    def share(s, step):
        for way, half in lanesets:
            hops = 4 - half if way == 0 else 3 + half
            if step > hops:
                continue
            if step:
                arriving[s, way, half, step - 1].wait_recv()
            if step < hops:
                chunk = ring(r - step if way == 0 else r + step, 8)
                ref = mine.at[s, chunk, pl.ds(128 * half, 128)]
                copy = send(
                    ref, ref, z_send.at[s, way, half, step], z_recv.at[s, way, half, step],
                    above if way == 0 else below,
                )
                arriving[s, way, half, step] = copy
                pending.append(copy)
            if step:
                across(s, (8 - step if way == 0 else step) % 8, half)
        if step == 0:
            for half in range(2):
                across(s, 0, half)

    row_copies = []

    def rows_out(s):
        for i in (2, 1, 3):
            copy = send(
                mine.at[s, r], row_in.at[s, k], r_send.at[s, i - 1], r_recv.at[s, i - 1], {"col": ring(k + i, 4)}
            )
            row_copies.append(copy)
            pending.append(copy)
        row_in[s, k] = mine[s, r]

    def write_basis(s):
        for slot in range(2):
            for half in range(2):
                value = jnp.zeros((128, 128), F32)
                for g in range(4):
                    wanted = owner_slot[4 * r + g] == 2 * c + slot
                    value = value + e_in[s][2 * g + half].astype(F32) * jnp.where(wanted, 1.0, 0.0)
                basis_out[slot, 0, pl.ds(128 * half, 128), pl.ds(128 * s, 128)] = value

    def weigh(s):
        total[s] = dot(held[k], mine[s, 2 * k]) + dot(held[4 + k], mine[s, 2 * k + 1])
        for i in (1, 3, 2):
            peer = ring(k + i, 4)
            for odd in range(2):
                for half in range(2):
                    pltpu.make_async_remote_copy(
                        src_ref=mine.at[s, 0, pl.ds(128 * half, 128)],
                        dst_ref=column_in.at[s, odd, peer, pl.ds(128 * half, 128)],
                        send_sem=y_send.at[s, 0, half],
                        recv_sem=y_recv.at[s, odd, peer, half],
                        device_id={"col": peer},
                        device_id_type=MESH,
                    ).wait_recv()
            total[s] += dot(held[peer], column_in[s, 0, peer]) + dot(held[4 + peer], column_in[s, 1, peer])

    def factor(value, part, actions):
        rows, marks = row_blocks(value), row_blocks(identity(1.0))
        for i in inverse_factor(rows, marks):
            if i in actions:
                actions[i]()
        for t in range(16):
            inverse[part, pl.ds(8 * t, 8)] = marks[t]

    factor(gram[0] + identity(SHIFT), 0, {})
    front[...] = dot(own[:, :128], inverse[0], ((1,), (1,)), HIGHEST)
    b_own[0] = front[...].astype(BF16)
    met(peers)
    spread(0)
    corner[...] = dot(gram[1], inverse[0], ((1,), (1,)), HIGHEST)

    def begin():
        select(0)
        share(0, 0)

    factor(
        gram[2] + identity(SHIFT) - dot(corner[...], corner[...], ((1,), (1,)), HIGHEST), 1, {11: begin}
    )
    rest = own[:, 128:] - dot(front[...], corner[...], ((1,), (1,)), HIGHEST)
    b_own[1] = dot(rest, inverse[1], ((1,), (1,)), HIGHEST).astype(BF16)
    spread(1)
    share(0, 1)
    write_basis(0)
    for load in loads:
        load.wait()
    select(1)
    share(1, 0)
    share(0, 2)
    share(1, 1)
    share(0, 3)
    write_basis(1)
    share(1, 2)
    share(0, 4)
    rows_out(0)
    share(1, 3)
    weigh(0)
    share(1, 4)
    rows_out(1)
    weigh(1)
    for copy in row_copies:
        copy.wait_recv()

    sums[...] = jnp.zeros_like(sums)
    for offset in range(8):
        rows = pl.ds(128 * offset, 128)
        value = jnp.concatenate([total[0, rows], total[1, rows]], axis=1)
        high = value.astype(BF16)
        low = (value - high.astype(F32)).astype(BF16)
        spot = pl.ds(128 * (offset % 2), 128)
        left = jnp.concatenate([row_in[0, offset // 2, spot], row_in[1, offset // 2, spot]], axis=1)
        product = dot(left, high, ((0,), (0,))) + dot(left, low, ((0,), (0,)))
        near = lax.rem(lax.shift_right_logical(block_map[c, 8 * r + offset], 3), 4)
        for g in range(4):
            sums[g] += product * jnp.where(near == g, 1.0, 0.0)

    copies = []
    for i in (2, 1, 3):
        peer = ring(k + i, 4)
        rows = pl.ds(pl.multiple_of(peer * 64, 64), 64)
        f_out[i - 1] = sums[:, rows].astype(BF16)
        copies.append(send(f_out.at[i - 1], f_in.at[i - 1], f_send.at[i - 1], f_recv.at[i - 1], {"col": peer}))
    value = sums[:, pl.ds(pl.multiple_of(k * 64, 64), 64)]
    for copy, i in zip(copies, (2, 1, 3)):
        copy.wait_recv()
        value = value + f_in[i - 1].astype(F32)
    pending += copies
    g_out[...] = value.astype(BF16).reshape(8, 32, 256)
    copies = []
    for i in (4, 3, 5, 2, 6, 1, 7):
        peer = ring(c + i, 8)
        copies.append(send(g_out.at[peer], g_in.at[c], g_send.at[i - 1], g_recv.at[i - 1], {"child": peer}))
    g_in[c] = g_out[c]
    for copy in copies:
        copy.wait_recv()
    pending += copies
    h_out[...] = jnp.sum(g_in[...].astype(F32), axis=0).astype(BF16)
    copies = []
    for i in (4, 3, 5, 2, 6, 1, 7):
        copies.append(send(h_out, h_in.at[c], h_send.at[i - 1], h_recv.at[i - 1], {"child": ring(c + i, 8)}))
    h_in[c] = h_out[...]
    for copy in copies:
        copy.wait_recv()
    pending += copies
    for slot in range(2):
        for half in range(2):
            value = jnp.zeros((32, 256), F32)
            for g in range(4):
                wanted = owner_slot[4 * r + g] == 2 * c + slot
                value = value + h_in[2 * g + half].astype(F32) * jnp.where(wanted, 1.0, 0.0)
            coupling_out[slot, 0, pl.ds(32 * half, 32)] = value
    for copy in pending:
        copy.wait_send()
    for peer, copy in forwards:
        pl.when(peer != k)(copy.wait_send)


def in_vmem():
    return pl.BlockSpec(memory_space=pltpu.VMEM)


def in_smem():
    return pl.BlockSpec(memory_space=pltpu.SMEM)


def sampled(schur, sketch, block_map):
    dma = pltpu.SemaphoreType.DMA
    return pl.pallas_call(
        sample_kernel,
        out_shape=(jax.ShapeDtypeStruct((128, 256), F32), jax.ShapeDtypeStruct((3, 128, 128), F32)),
        in_specs=[pl.BlockSpec(memory_space=pl.ANY), in_vmem(), in_smem()],
        out_specs=(in_vmem(), in_vmem()),
        scratch_shapes=[
            pltpu.VMEM((8, 1024, 256), BF16),
            pltpu.VMEM((256, 1024), BF16),
            pltpu.VMEM((8, 256, 256), F32),
            pltpu.VMEM((2, 2, 2, 4, 64, 256), BF16),
            pltpu.VMEM((2, 2, 2, 4, 64, 256), BF16),
            pltpu.VMEM((2, 8, 128, 256), BF16),
            pltpu.VMEM((2, 1024, 128), F32),
            pltpu.VMEM((2, 3, 256, 128), BF16),
            pltpu.VMEM((2, 3, 256, 128), BF16),
            pltpu.VMEM((2, 2, 128, 128), BF16),
            pltpu.VMEM((2, 8, 128, 128), BF16),
            pltpu.VMEM((2, 8, 128, 128), BF16),
            dma((8,)),
            dma((2, 2, 2, 4)), dma((2, 2, 2, 4)),
            dma((2, 2, 2, 4)), dma((2, 2, 2, 4)),
            dma((2, 3)), dma((2, 3)),
            dma((2, 7)), dma((2, 7)),
            dma((2, 8)), dma((2, 8)),
        ],
        compiler_params=pltpu.CompilerParams(
            collective_id=0, has_side_effects=True, vmem_limit_bytes=VMEM_LIMIT
        ),
        name="samples",
    )(schur, sketch, block_map)


def coupled(schur, own, gram, block_map, owner_slot):
    dma = pltpu.SemaphoreType.DMA
    return pl.pallas_call(
        coupling_kernel,
        out_shape=(
            jax.ShapeDtypeStruct((2, 1, 256, 256), F32),
            jax.ShapeDtypeStruct((2, 1, 64, 256), F32),
        ),
        in_specs=[pl.BlockSpec(memory_space=pl.ANY), in_vmem(), in_vmem(), in_smem(), in_smem()],
        out_specs=(in_vmem(), in_vmem()),
        scratch_shapes=[
            pltpu.VMEM((8, 1024, 256), BF16),
            pltpu.VMEM((2, 128, 128), F32),
            pltpu.VMEM((128, 128), F32),
            pltpu.VMEM((128, 128), F32),
            pltpu.VMEM((2, 128, 128), BF16),
            pltpu.VMEM((8, 128, 128), BF16),
            pltpu.VMEM((8, 128, 128), BF16),
            pltpu.VMEM((2, 8, 256, 128), BF16),
            pltpu.VMEM((2, 2, 4, 256, 128), BF16),
            pltpu.VMEM((2, 4, 256, 128), BF16),
            pltpu.VMEM((2, 1024, 128), F32),
            pltpu.VMEM((4, 256, 256), F32),
            pltpu.VMEM((3, 4, 64, 256), BF16),
            pltpu.VMEM((3, 4, 64, 256), BF16),
            pltpu.VMEM((8, 32, 256), BF16),
            pltpu.VMEM((8, 32, 256), BF16),
            pltpu.VMEM((32, 256), BF16),
            pltpu.VMEM((8, 32, 256), BF16),
            dma((8,)),
            dma((2, 7)), dma((2, 7)),
            dma((2, 2, 2, 4)), dma((2, 2, 2, 4)),
            dma((2, 8, 2)), dma((2, 2, 4, 2)),
            dma((2, 3)), dma((2, 3)),
            dma((3,)), dma((3,)),
            dma((7,)), dma((7,)),
            dma((7,)), dma((7,)),
        ],
        compiler_params=pltpu.CompilerParams(
            collective_id=1, has_side_effects=True, vmem_limit_bytes=VMEM_LIMIT
        ),
        name="coupling",
    )(schur, own, gram, block_map, owner_slot)


def shards(schur_blocks, sketch_cols, block_map, owner_slot):
    own, gram = sampled(schur_blocks, sketch_cols, block_map)
    return coupled(schur_blocks, own, gram, block_map, owner_slot)


def solution(mesh):
    placed = (P("child", "row", "col"), P("row", None), P(), P())
    return jax.shard_map(
        shards,
        mesh=mesh,
        in_specs=placed,
        out_specs=(P("child", "row", "col", None), P("child", "row", "col", None)),
        check_vma=False,
    )
```

time: 189 us -> 124 us (0.66)
  other arithmetic: 54.6 us -> 0 us
  local copies, waits for them, and re-layouts: 9.43 us -> 3.44 us
    another operation x9 -> x0, other arithmetic: 53.9 us -> none  [the longest x6 34.2 us: orthonormal(): factor = jnp.linalg.cholesky(gram + SHIFT * jnp.eye(256, dtype=F32))]
    pallas_call x1, Pallas kernels: 66.1 us -> 58.5 us  [sampled(): pl.pallas_call(sample_kernel, out_shape=(jax.ShapeDtypeStruct((128, 256),...]
    pallas_call x1, Pallas kernels: 55.1 us -> 61.4 us  [coupled(): pl.pallas_call(coupling_kernel, out_shape=(jax.ShapeDtypeStruct((2, 1, 25...]
    another operation x19 -> x0, local copies, waits for them, and re-layouts: 4.75 us -> none
where the time goes in v3:
time: 124 us
  Pallas kernels  120 us (97%)
  local copies, waits for them, and re-layouts  3.44 us (3%)
    pallas_call x1, Pallas kernels, coupled(): pl.pallas_call(coupling_kernel, out_shape=(jax.ShapeDtypeStruct((2, 1, 25...  61.4 us
    pallas_call x1, Pallas kernels, sampled(): pl.pallas_call(sample_kernel, out_shape=(jax.ShapeDtypeStruct((128, 256),...  58.5 us
    unnamed x2, local copies, waits for them, and re-layouts  3.44 us

profile of v3, /device:TPU:1, one launch (start us, length us, event | category | flops | bytes accessed | tf_op | source)
XLA Modules:
  0.0 123.9 jit_solution(12590332166421039649)
XLA Ops:
  0.6 58.5 %samples.1 = (f32[128,256]{1,0:T(8,128)}, f32[3,128,128]{2,1,0:T(8,128)}) custom-call(bf16[1,1024,2048]{2,1,0:T(8,128)(2,1)} %schur.3, bf16[1024,256]{1,0:T(8,128)(2,1)} %sketch.1, s32[8,64]{1,0:T(8,128)} %block_map.3), custom_call_target="tpu_custom_call" | custom-call | tf_op jit(solution)/shard_map/samples/pallas_call | solution.py:508
  59.1 61.4 %coupling.1 = (f32[2,1,256,256]{3,2,1,0:T(8,128)}, f32[2,1,64,256]{3,2,1,0:T(8,128)}) custom-call(bf16[1,1024,2048]{2,1,0:T(8,128)(2,1)} %schur.3, f32[128,256]{1,0:T(8,128)} %get-tuple-element.4.own, f32[3,128,128]{2,1,0:T(8,128)} %get-tuple-element.5.gram, s32[8,64]{1,0:T(8,128)} %block_map.3, s32[32]{0:T(128)} %owner_slot.1), custom_call_target="tpu_custom_call" | custom-call | tf_op jit(solution)/shard_map/coupling/pallas_call | solution.py:542
  120.5 1.9 %copy.8 = f32[2,1,256,256]{3,2,1,0:T(8,128)} copy(f32[2,1,256,256]{3,2,1,0:T(8,128)} %get-tuple-element.8) | data formatting | bytes 1048576
  122.4 1.6 %copy.9 = f32[2,1,64,256]{3,2,1,0:T(8,128)} copy(f32[2,1,64,256]{3,2,1,0:T(8,128)} %get-tuple-element.9) | data formatting | bytes 262144

commit v4 on v3

--- a/solution.py
+++ b/solution.py
@@ -283,11 +283,11 @@
 
 
 def coupling_kernel(
-    schur, own, gram, block_map, owner_slot, basis_out, coupling_out,
+    schur, own, gram, block_map, basis_out, coupling_out,
     held, inverse, corner, front, b_own, e_low, e_high, mine, column_in, row_in, total, sums,
-    f_out, f_in, g_out, g_in, h_out, h_in,
-    load_sem, e_send, e_recv, z_send, z_recv, y_send, y_recv, r_send, r_recv, f_send, f_recv, g_send, g_recv,
-    h_send, h_recv,
+    f_out, f_in, x_out, x_in, g_out, g_in, v_sum, v_out, v_in, h_out, h_in,
+    load_sem, e_send, e_recv, z_send, z_recv, y_send, y_recv, r_send, r_recv, f_send, f_recv, x_send, x_recv,
+    g_send, g_recv, v_send, v_recv, h_send, h_recv,
 ):
     c, r, k = place()
     below, above = {"row": ring(r - 1, 8)}, {"row": ring(r + 1, 8)}
@@ -371,13 +371,7 @@
         row_in[s, k] = mine[s, r]
 
     def write_basis(s):
-        for slot in range(2):
-            for half in range(2):
-                value = jnp.zeros((128, 128), F32)
-                for g in range(4):
-                    wanted = owner_slot[4 * r + g] == 2 * c + slot
-                    value = value + e_in[s][2 * g + half].astype(F32) * jnp.where(wanted, 1.0, 0.0)
-                basis_out[slot, 0, pl.ds(128 * half, 128), pl.ds(128 * s, 128)] = value
+        basis_out[s] = e_in[s][...]
 
     def weigh(s):
         total[s] = dot(held[k], mine[s, 2 * k]) + dot(held[4 + k], mine[s, 2 * k + 1])
@@ -454,27 +448,50 @@
         for g in range(4):
             sums[g] += product * jnp.where(near == g, 1.0, 0.0)
 
+    for g in range(2):
+        quarters = sums[2 + g].astype(BF16).reshape(4, 4, 16, 256)
+        for q in range(4):
+            x_out[4 * g + q] = quarters[:, q]
+    x_copies, copies = [], []
+    for i in (2, 1, 3):
+        peer = ring(k + i, 4)
+        rows = pl.ds(pl.multiple_of(peer * 64, 64), 64)
+        f_out[i - 1] = sums[:2, rows].astype(BF16)
+        copies.append(send(f_out.at[i - 1], f_in.at[i - 1], f_send.at[i - 1], f_recv.at[i - 1], {"col": peer}))
+    for i in (4, 3, 5, 2, 6, 1, 7):
+        peer = ring(c + i, 8)
+        x_copies.append(send(x_out.at[peer], x_in.at[c], x_send.at[i - 1], x_recv.at[i - 1], {"child": peer}))
+    x_in[c] = x_out[c]
+    value = sums[:2, pl.ds(pl.multiple_of(k * 64, 64), 64)]
+    for copy, i in zip(copies, (2, 1, 3)):
+        copy.wait_recv()
+        value = value + f_in[i - 1].astype(F32)
+    pending += copies
+    g_out[...] = value.astype(BF16).reshape(8, 16, 256)
+    g_copies = []
+    for i in (4, 3, 5, 2, 6, 1, 7):
+        peer = ring(c + i, 8)
+        g_copies.append(send(g_out.at[peer], g_in.at[c], g_send.at[i - 1], g_recv.at[i - 1], {"child": peer}))
+    g_in[c] = g_out[c]
+    for copy in x_copies:
+        copy.wait_recv()
+    pending += x_copies
+    v_sum[...] = jnp.sum(x_in[...].astype(F32), axis=0)
+    v_out[...] = v_sum[...].astype(BF16)
     copies = []
     for i in (2, 1, 3):
         peer = ring(k + i, 4)
-        rows = pl.ds(pl.multiple_of(peer * 64, 64), 64)
-        f_out[i - 1] = sums[:, rows].astype(BF16)
-        copies.append(send(f_out.at[i - 1], f_in.at[i - 1], f_send.at[i - 1], f_recv.at[i - 1], {"col": peer}))
-    value = sums[:, pl.ds(pl.multiple_of(k * 64, 64), 64)]
+        copies.append(send(v_out.at[peer], v_in.at[i - 1], v_send.at[i - 1], v_recv.at[i - 1], {"col": peer}))
+    for copy in g_copies:
+        copy.wait_recv()
+    pending += g_copies
+    h_out[0] = jnp.sum(g_in[...].astype(F32), axis=0).astype(BF16)
+    value = v_sum[k]
     for copy, i in zip(copies, (2, 1, 3)):
         copy.wait_recv()
-        value = value + f_in[i - 1].astype(F32)
+        value = value + v_in[i - 1].astype(F32)
     pending += copies
-    g_out[...] = value.astype(BF16).reshape(8, 32, 256)
-    copies = []
-    for i in (4, 3, 5, 2, 6, 1, 7):
-        peer = ring(c + i, 8)
-        copies.append(send(g_out.at[peer], g_in.at[c], g_send.at[i - 1], g_recv.at[i - 1], {"child": peer}))
-    g_in[c] = g_out[c]
-    for copy in copies:
-        copy.wait_recv()
-    pending += copies
-    h_out[...] = jnp.sum(g_in[...].astype(F32), axis=0).astype(BF16)
+    h_out[1] = value.astype(BF16)
     copies = []
     for i in (4, 3, 5, 2, 6, 1, 7):
         copies.append(send(h_out, h_in.at[c], h_send.at[i - 1], h_recv.at[i - 1], {"child": ring(c + i, 8)}))
@@ -482,13 +499,7 @@
     for copy in copies:
         copy.wait_recv()
     pending += copies
-    for slot in range(2):
-        for half in range(2):
-            value = jnp.zeros((32, 256), F32)
-            for g in range(4):
-                wanted = owner_slot[4 * r + g] == 2 * c + slot
-                value = value + h_in[2 * g + half].astype(F32) * jnp.where(wanted, 1.0, 0.0)
-            coupling_out[slot, 0, pl.ds(32 * half, 32)] = value
+    coupling_out[...] = h_in[...]
     for copy in pending:
         copy.wait_send()
     for peer, copy in forwards:
@@ -537,15 +548,15 @@
     )(schur, sketch, block_map)
 
 
-def coupled(schur, own, gram, block_map, owner_slot):
+def coupled(schur, own, gram, block_map):
     dma = pltpu.SemaphoreType.DMA
     return pl.pallas_call(
         coupling_kernel,
         out_shape=(
-            jax.ShapeDtypeStruct((2, 1, 256, 256), F32),
-            jax.ShapeDtypeStruct((2, 1, 64, 256), F32),
+            jax.ShapeDtypeStruct((2, 8, 128, 128), BF16),
+            jax.ShapeDtypeStruct((8, 2, 16, 256), BF16),
         ),
-        in_specs=[pl.BlockSpec(memory_space=pl.ANY), in_vmem(), in_vmem(), in_smem(), in_smem()],
+        in_specs=[pl.BlockSpec(memory_space=pl.ANY), in_vmem(), in_vmem(), in_smem()],
         out_specs=(in_vmem(), in_vmem()),
         scratch_shapes=[
             pltpu.VMEM((8, 1024, 256), BF16),
@@ -560,12 +571,17 @@
             pltpu.VMEM((2, 4, 256, 128), BF16),
             pltpu.VMEM((2, 1024, 128), F32),
             pltpu.VMEM((4, 256, 256), F32),
-            pltpu.VMEM((3, 4, 64, 256), BF16),
-            pltpu.VMEM((3, 4, 64, 256), BF16),
-            pltpu.VMEM((8, 32, 256), BF16),
-            pltpu.VMEM((8, 32, 256), BF16),
-            pltpu.VMEM((32, 256), BF16),
-            pltpu.VMEM((8, 32, 256), BF16),
+            pltpu.VMEM((3, 2, 64, 256), BF16),
+            pltpu.VMEM((3, 2, 64, 256), BF16),
+            pltpu.VMEM((8, 4, 16, 256), BF16),
+            pltpu.VMEM((8, 4, 16, 256), BF16),
+            pltpu.VMEM((8, 16, 256), BF16),
+            pltpu.VMEM((8, 16, 256), BF16),
+            pltpu.VMEM((4, 16, 256), F32),
+            pltpu.VMEM((4, 16, 256), BF16),
+            pltpu.VMEM((3, 16, 256), BF16),
+            pltpu.VMEM((2, 16, 256), BF16),
+            pltpu.VMEM((8, 2, 16, 256), BF16),
             dma((8,)),
             dma((2, 7)), dma((2, 7)),
             dma((2, 2, 2, 4)), dma((2, 2, 2, 4)),
@@ -574,17 +590,50 @@
             dma((3,)), dma((3,)),
             dma((7,)), dma((7,)),
             dma((7,)), dma((7,)),
+            dma((3,)), dma((3,)),
+            dma((7,)), dma((7,)),
         ],
         compiler_params=pltpu.CompilerParams(
             collective_id=1, has_side_effects=True, vmem_limit_bytes=VMEM_LIMIT
         ),
         name="coupling",
-    )(schur, own, gram, block_map, owner_slot)
+    )(schur, own, gram, block_map)
+
+
+def place_kernel(basis, coupling, owner_slot, basis_out, coupling_out):
+    c, r = lax.axis_index("child"), lax.axis_index("row")
+    for slot in range(2):
+        share = [jnp.where(owner_slot[4 * r + g] == 2 * c + slot, 1.0, 0.0) for g in range(4)]
+        for half in range(2):
+            for s in range(2):
+                value = basis[s, half].astype(F32) * share[0]
+                for g in range(1, 4):
+                    value = value + basis[s, 2 * g + half].astype(F32) * share[g]
+                basis_out[slot, 0, pl.ds(128 * half, 128), pl.ds(128 * s, 128)] = value
+        for q in range(4):
+            value = coupling[q, 0].astype(F32) * share[0]
+            for g in range(1, 4):
+                value = value + coupling[4 * (g % 2) + q, g // 2].astype(F32) * share[g]
+            coupling_out[slot, 0, pl.ds(16 * q, 16)] = value
+
+
+def placed_results(basis, coupling, owner_slot):
+    return pl.pallas_call(
+        place_kernel,
+        out_shape=(
+            jax.ShapeDtypeStruct((2, 1, 256, 256), F32),
+            jax.ShapeDtypeStruct((2, 1, 64, 256), F32),
+        ),
+        in_specs=[in_vmem(), in_vmem(), in_smem()],
+        out_specs=(in_vmem(), in_vmem()),
+        name="results",
+    )(basis, coupling, owner_slot)
 
 
 def shards(schur_blocks, sketch_cols, block_map, owner_slot):
     own, gram = sampled(schur_blocks, sketch_cols, block_map)
-    return coupled(schur_blocks, own, gram, block_map, owner_slot)
+    basis, coupling = coupled(schur_blocks, own, gram, block_map)
+    return placed_results(basis, coupling, owner_slot)
 
 
 def solution(mesh):

time: 124 us -> 120 us (0.968)
  local copies, waits for them, and re-layouts: 3.44 us -> 0 us
    unnamed x2 -> x0, local copies, waits for them, and re-layouts: 3.44 us -> none
    pallas_call x1 -> x2, Pallas kernels: 61.4 us -> 60.3 us  [the longest x1 58.2 us: coupled(): pl.pallas_call(coupling_kernel, out_shape=(jax.ShapeDtypeStruct((2, 8, 12...]
where the time goes in v4:
time: 120 us; the launch traced here: 119 us
  Pallas kernels  119 us (99%)
    pallas_call x1, Pallas kernels, sampled(): pl.pallas_call(sample_kernel, out_shape=(jax.ShapeDtypeStruct((128, 256),...  58.5 us
    pallas_call x1, Pallas kernels, coupled(): pl.pallas_call(coupling_kernel, out_shape=(jax.ShapeDtypeStruct((2, 8, 12...  58.2 us

profile of v4, /device:TPU:1, one launch (start us, length us, event | category | flops | bytes accessed | tf_op | source)
XLA Modules:
  0.0 119.4 jit_solution(17451380445926403075)
XLA Ops:
  0.6 58.5 %samples.1 = (f32[128,256]{1,0:T(8,128)}, f32[3,128,128]{2,1,0:T(8,128)}) custom-call(bf16[1,1024,2048]{2,1,0:T(8,128)(2,1)} %schur.3, bf16[1024,256]{1,0:T(8,128)(2,1)} %sketch.1, s32[8,64]{1,0:T(8,128)} %block_map.3), custom_call_target="tpu_custom_call" | custom-call | tf_op jit(solution)/shard_map/samples/pallas_call | solution.py:519
  59.1 58.2 %coupling.1 = (bf16[2,8,128,128]{3,2,1,0:T(8,128)(2,1)}, bf16[8,2,16,256]{3,2,1,0:T(8,128)(2,1)}) custom-call(bf16[1,1024,2048]{2,1,0:T(8,128)(2,1)} %schur.3, f32[128,256]{1,0:T(8,128)} %get-tuple-element.6.own, f32[3,128,128]{2,1,0:T(8,128)} %get-tuple-element.7.gram, s32[8,64]{1,0:T(8,128)} %block_map.3), custom_call_target="tpu_custom_call" | custom-call | tf_op jit(solution)/shard_map/coupling/pallas_call | solution.py:553
  117.3 2.1 %results.1 = (f32[2,1,256,256]{3,2,1,0:T(8,128)}, f32[2,1,64,256]{3,2,1,0:T(8,128)}) custom-call(bf16[2,8,128,128]{3,2,1,0:T(8,128)(2,1)} %get-tuple-element.8.basis, bf16[8,2,16,256]{3,2,1,0:T(8,128)(2,1)} %get-tuple-element.9.coupling, s32[32]{0:T(128)} %owner_slot.1), custom_call_target="tpu_custom_call" | custom-call | tf_op jit(solution)/shard_map/results/pallas_call | solution.py:621

commit v5 on v4

--- a/solution.py
+++ b/solution.py
@@ -373,8 +373,10 @@
     def write_basis(s):
         basis_out[s] = e_in[s][...]
 
+    def weigh_own(s):
+        total[s] = dot(held[k], mine[s, 2 * k]) + dot(held[4 + k], mine[s, 2 * k + 1])
+
     def weigh(s):
-        total[s] = dot(held[k], mine[s, 2 * k]) + dot(held[4 + k], mine[s, 2 * k + 1])
         for i in (1, 3, 2):
             peer = ring(k + i, 4)
             for odd in range(2):
@@ -407,30 +409,34 @@
     def begin():
         select(0)
         share(0, 0)
+        rows_out(0)
+
+    def relay():
+        share(0, 1)
 
     factor(
-        gram[2] + identity(SHIFT) - dot(corner[...], corner[...], ((1,), (1,)), HIGHEST), 1, {11: begin}
+        gram[2] + identity(SHIFT) - dot(corner[...], corner[...], ((1,), (1,)), HIGHEST), 1, {10: begin, 15: relay}
     )
     rest = own[:, 128:] - dot(front[...], corner[...], ((1,), (1,)), HIGHEST)
     b_own[1] = dot(rest, inverse[1], ((1,), (1,)), HIGHEST).astype(BF16)
     spread(1)
-    share(0, 1)
+    share(0, 2)
     write_basis(0)
+    select(1)
+    share(1, 0)
+    rows_out(1)
+    share(0, 3)
+    share(1, 1)
+    share(0, 4)
+    share(1, 2)
+    write_basis(1)
     for load in loads:
         load.wait()
-    select(1)
-    share(1, 0)
-    share(0, 2)
-    share(1, 1)
-    share(0, 3)
-    write_basis(1)
-    share(1, 2)
-    share(0, 4)
-    rows_out(0)
     share(1, 3)
+    weigh_own(0)
+    share(1, 4)
+    weigh_own(1)
     weigh(0)
-    share(1, 4)
-    rows_out(1)
     weigh(1)
     for copy in row_copies:
         copy.wait_recv()

time: 120 us -> 117 us (0.975)
  Pallas kernels: 119 us -> 116 us
    pallas_call x1, Pallas kernels: 58.2 us -> 55.4 us  [coupled(): pl.pallas_call(coupling_kernel, out_shape=(jax.ShapeDtypeStruct((2, 8, 12...]
where the time goes in v5:
time: 117 us
  Pallas kernels  116 us (99%)
    pallas_call x1, Pallas kernels, sampled(): pl.pallas_call(sample_kernel, out_shape=(jax.ShapeDtypeStruct((128, 256),...  58.5 us
    pallas_call x1, Pallas kernels, coupled(): pl.pallas_call(coupling_kernel, out_shape=(jax.ShapeDtypeStruct((2, 8, 12...  55.4 us

profile of v5, /device:TPU:1, one launch (start us, length us, event | category | flops | bytes accessed | tf_op | source)
XLA Modules:
  0.0 116.6 jit_solution(9728023107015180103)
XLA Ops:
  0.6 58.5 %samples.1 = (f32[128,256]{1,0:T(8,128)}, f32[3,128,128]{2,1,0:T(8,128)}) custom-call(bf16[1,1024,2048]{2,1,0:T(8,128)(2,1)} %schur.3, bf16[1024,256]{1,0:T(8,128)(2,1)} %sketch.1, s32[8,64]{1,0:T(8,128)} %block_map.3), custom_call_target="tpu_custom_call" | custom-call | tf_op jit(solution)/shard_map/samples/pallas_call | solution.py:525
  59.1 55.4 %coupling.1 = (bf16[2,8,128,128]{3,2,1,0:T(8,128)(2,1)}, bf16[8,2,16,256]{3,2,1,0:T(8,128)(2,1)}) custom-call(bf16[1,1024,2048]{2,1,0:T(8,128)(2,1)} %schur.3, f32[128,256]{1,0:T(8,128)} %get-tuple-element.6.own, f32[3,128,128]{2,1,0:T(8,128)} %get-tuple-element.7.gram, s32[8,64]{1,0:T(8,128)} %block_map.3), custom_call_target="tpu_custom_call" | custom-call | tf_op jit(solution)/shard_map/coupling/pallas_call | solution.py:559
  114.5 2.1 %results.1 = (f32[2,1,256,256]{3,2,1,0:T(8,128)}, f32[2,1,64,256]{3,2,1,0:T(8,128)}) custom-call(bf16[2,8,128,128]{3,2,1,0:T(8,128)(2,1)} %get-tuple-element.8.basis, bf16[8,2,16,256]{3,2,1,0:T(8,128)(2,1)} %get-tuple-element.9.coupling, s32[32]{0:T(128)} %owner_slot.1), custom_call_target="tpu_custom_call" | custom-call | tf_op jit(solution)/shard_map/results/pallas_call | solution.py:627

commit v6 on v5

--- a/solution.py
+++ b/solution.py
@@ -104,7 +104,7 @@
     return jnp.where(row == column, scale, 0.0)
 
 
-def sample_kernel(
+def sample_steps(
     schur, sketch, block_map, own_out, gram_out,
     held, turned, part, sums_out, sums_in, power, total, b_out, b_in, c_out, c_in, z_all,
     load_sem, a_send, a_recv, p_send, p_recv, b_send, b_recv, c_send, c_recv, z_send, z_recv,
@@ -273,6 +273,7 @@
         copy.wait_recv()
     first = z_all[0].reshape(1024, 128)
     gram_out[0] = dot(first, first, ((0,), (0,)))
+    yield
     for copy in gathered[1]:
         copy.wait_recv()
     second = z_all[1].reshape(1024, 128)
@@ -282,22 +283,15 @@
         copy.wait_send()
 
 
-def coupling_kernel(
-    schur, own, gram, block_map, basis_out, coupling_out,
+def coupling_steps(
+    sampling, own, gram, block_map, basis_out, coupling_out,
     held, inverse, corner, front, b_own, e_low, e_high, mine, column_in, row_in, total, sums,
     f_out, f_in, x_out, x_in, g_out, g_in, v_sum, v_out, v_in, h_out, h_in,
-    load_sem, e_send, e_recv, z_send, z_recv, y_send, y_recv, r_send, r_recv, f_send, f_recv, x_send, x_recv,
+    e_send, e_recv, z_send, z_recv, y_send, y_recv, r_send, r_recv, f_send, f_recv, x_send, x_recv,
     g_send, g_recv, v_send, v_recv, h_send, h_recv,
 ):
     c, r, k = place()
     below, above = {"row": ring(r - 1, 8)}, {"row": ring(r + 1, 8)}
-    siblings = [{"child": ring(c + i, 8)} for i in range(1, 8)]
-    peers = [below, above] + siblings + [{"col": ring(k + i, 4)} for i in range(1, 4)]
-    hello(peers)
-    loads = []
-    for chunk in range(8):
-        loads.append(pltpu.make_async_copy(schur.at[0, :, columns(chunk)], held.at[chunk], load_sem.at[chunk]))
-        loads[-1].start()
     pending = []
     outgoing = {}
     e_in = (e_low, e_high)
@@ -402,8 +396,9 @@
     factor(gram[0] + identity(SHIFT), 0, {})
     front[...] = dot(own[:, :128], inverse[0], ((1,), (1,)), HIGHEST)
     b_own[0] = front[...].astype(BF16)
-    met(peers)
     spread(0)
+    for _ in sampling:
+        pass
     corner[...] = dot(gram[1], inverse[0], ((1,), (1,)), HIGHEST)
 
     def begin():
@@ -430,8 +425,6 @@
     share(0, 4)
     share(1, 2)
     write_basis(1)
-    for load in loads:
-        load.wait()
     share(1, 3)
     weigh_own(0)
     share(1, 4)
@@ -512,6 +505,12 @@
         pl.when(peer != k)(copy.wait_send)
 
 
+def whole_kernel(schur, sketch, block_map, basis_out, coupling_out, own, gram, held, *rest):
+    sampling = sample_steps(schur, sketch, block_map, own, gram, held, *rest[:22])
+    next(sampling)
+    coupling_steps(sampling, own, gram, block_map, basis_out, coupling_out, held, *rest[22:])
+
+
 def in_vmem():
     return pl.BlockSpec(memory_space=pltpu.VMEM)
 
@@ -520,14 +519,19 @@
     return pl.BlockSpec(memory_space=pltpu.SMEM)
 
 
-def sampled(schur, sketch, block_map):
+def solved(schur, sketch, block_map):
     dma = pltpu.SemaphoreType.DMA
     return pl.pallas_call(
-        sample_kernel,
-        out_shape=(jax.ShapeDtypeStruct((128, 256), F32), jax.ShapeDtypeStruct((3, 128, 128), F32)),
+        whole_kernel,
+        out_shape=(
+            jax.ShapeDtypeStruct((2, 8, 128, 128), BF16),
+            jax.ShapeDtypeStruct((8, 2, 16, 256), BF16),
+        ),
         in_specs=[pl.BlockSpec(memory_space=pl.ANY), in_vmem(), in_smem()],
         out_specs=(in_vmem(), in_vmem()),
         scratch_shapes=[
+            pltpu.VMEM((128, 256), F32),
+            pltpu.VMEM((3, 128, 128), F32),
             pltpu.VMEM((8, 1024, 256), BF16),
             pltpu.VMEM((256, 1024), BF16),
             pltpu.VMEM((8, 256, 256), F32),
@@ -546,26 +550,6 @@
             dma((2, 3)), dma((2, 3)),
             dma((2, 7)), dma((2, 7)),
             dma((2, 8)), dma((2, 8)),
-        ],
-        compiler_params=pltpu.CompilerParams(
-            collective_id=0, has_side_effects=True, vmem_limit_bytes=VMEM_LIMIT
-        ),
-        name="samples",
-    )(schur, sketch, block_map)
-
-
-def coupled(schur, own, gram, block_map):
-    dma = pltpu.SemaphoreType.DMA
-    return pl.pallas_call(
-        coupling_kernel,
-        out_shape=(
-            jax.ShapeDtypeStruct((2, 8, 128, 128), BF16),
-            jax.ShapeDtypeStruct((8, 2, 16, 256), BF16),
-        ),
-        in_specs=[pl.BlockSpec(memory_space=pl.ANY), in_vmem(), in_vmem(), in_smem()],
-        out_specs=(in_vmem(), in_vmem()),
-        scratch_shapes=[
-            pltpu.VMEM((8, 1024, 256), BF16),
             pltpu.VMEM((2, 128, 128), F32),
             pltpu.VMEM((128, 128), F32),
             pltpu.VMEM((128, 128), F32),
@@ -588,7 +572,6 @@
             pltpu.VMEM((3, 16, 256), BF16),
             pltpu.VMEM((2, 16, 256), BF16),
             pltpu.VMEM((8, 2, 16, 256), BF16),
-            dma((8,)),
             dma((2, 7)), dma((2, 7)),
             dma((2, 2, 2, 4)), dma((2, 2, 2, 4)),
             dma((2, 8, 2)), dma((2, 2, 4, 2)),
@@ -600,10 +583,10 @@
             dma((7,)), dma((7,)),
         ],
         compiler_params=pltpu.CompilerParams(
-            collective_id=1, has_side_effects=True, vmem_limit_bytes=VMEM_LIMIT
+            collective_id=0, has_side_effects=True, vmem_limit_bytes=VMEM_LIMIT
         ),
-        name="coupling",
-    )(schur, own, gram, block_map)
+        name="basis_step",
+    )(schur, sketch, block_map)
 
 
 def place_kernel(basis, coupling, owner_slot, basis_out, coupling_out):
@@ -637,8 +620,7 @@
 
 
 def shards(schur_blocks, sketch_cols, block_map, owner_slot):
-    own, gram = sampled(schur_blocks, sketch_cols, block_map)
-    basis, coupling = coupled(schur_blocks, own, gram, block_map)
+    basis, coupling = solved(schur_blocks, sketch_cols, block_map)
     return placed_results(basis, coupling, owner_slot)
 
 

time: 117 us -> 114 us (0.974)
  Pallas kernels: 116 us -> 113 us
    pallas_call x2 -> x1, Pallas kernels: 114 us -> 111 us  [solved(): pl.pallas_call(whole_kernel, out_shape=(jax.ShapeDtypeStruct((2, 8, 128,...]
where the time goes in v6:
time: 114 us
  Pallas kernels  113 us (99%)
    pallas_call x1, Pallas kernels, solved(): pl.pallas_call(whole_kernel, out_shape=(jax.ShapeDtypeStruct((2, 8, 128,...  111 us

profile of v6, /device:TPU:1, one launch (start us, length us, event | category | flops | bytes accessed | tf_op | source)
XLA Modules:
  0.0 113.5 jit_solution(3557055527182804163)
XLA Ops:
  0.6 110.8 %basis_step.1 = (bf16[2,8,128,128]{3,2,1,0:T(8,128)(2,1)}, bf16[8,2,16,256]{3,2,1,0:T(8,128)(2,1)}) custom-call(bf16[1,1024,2048]{2,1,0:T(8,128)(2,1)} %schur.1, bf16[1024,256]{1,0:T(8,128)(2,1)} %sketch.1, s32[8,64]{1,0:T(8,128)} %block_map.1), custom_call_target="tpu_custom_call" | custom-call | tf_op jit(solution)/shard_map/basis_step/pallas_call | solution.py:524
  111.4 2.1 %results.1 = (f32[2,1,256,256]{3,2,1,0:T(8,128)}, f32[2,1,64,256]{3,2,1,0:T(8,128)}) custom-call(bf16[2,8,128,128]{3,2,1,0:T(8,128)(2,1)} %get-tuple-element.4.basis, bf16[8,2,16,256]{3,2,1,0:T(8,128)(2,1)} %get-tuple-element.5.coupling, s32[32]{0:T(128)} %owner_slot.1), custom_call_target="tpu_custom_call" | custom-call | tf_op jit(solution)/shard_map/results/pallas_call | solution.py:610

commit v7 on v6

--- a/solution.py
+++ b/solution.py
@@ -349,9 +349,6 @@
                 pending.append(copy)
             if step:
                 across(s, (8 - step if way == 0 else step) % 8, half)
-        if step == 0:
-            for half in range(2):
-                across(s, 0, half)
 
     row_copies = []
 
@@ -371,18 +368,25 @@
         total[s] = dot(held[k], mine[s, 2 * k]) + dot(held[4 + k], mine[s, 2 * k + 1])
 
     def weigh(s):
+        for copy in row_copies[3 * s : 3 * s + 3]:
+            copy.wait_recv()
         for i in (1, 3, 2):
             peer = ring(k + i, 4)
             for odd in range(2):
+                @pl.when(2 * k + odd == r)
+                def _():
+                    column_in[s, odd, peer] = row_in[s, peer]
+
                 for half in range(2):
-                    pltpu.make_async_remote_copy(
+                    arrival = pltpu.make_async_remote_copy(
                         src_ref=mine.at[s, 0, pl.ds(128 * half, 128)],
                         dst_ref=column_in.at[s, odd, peer, pl.ds(128 * half, 128)],
                         send_sem=y_send.at[s, 0, half],
                         recv_sem=y_recv.at[s, odd, peer, half],
                         device_id={"col": peer},
                         device_id_type=MESH,
-                    ).wait_recv()
+                    )
+                    pl.when(2 * k + odd != r)(arrival.wait_recv)
             total[s] += dot(held[peer], column_in[s, 0, peer]) + dot(held[4 + peer], column_in[s, 1, peer])
 
     def factor(value, part, actions):
@@ -431,8 +435,6 @@
     weigh_own(1)
     weigh(0)
     weigh(1)
-    for copy in row_copies:
-        copy.wait_recv()
 
     sums[...] = jnp.zeros_like(sums)
     for offset in range(8):

time: 114 us -> 113 us (level)
  no operation moved by 1% of the time
where the time goes in v7:
time: 113 us
  Pallas kernels  112 us (99%)
    pallas_call x1, Pallas kernels, solved(): pl.pallas_call(whole_kernel, out_shape=(jax.ShapeDtypeStruct((2, 8, 128,...  110 us

profile of v7, /device:TPU:1, one launch (start us, length us, event | category | flops | bytes accessed | tf_op | source)
XLA Modules:
  0.0 113.0 jit_solution(17844797815464510170)
XLA Ops:
  0.6 110.3 %basis_step.1 = (bf16[2,8,128,128]{3,2,1,0:T(8,128)(2,1)}, bf16[8,2,16,256]{3,2,1,0:T(8,128)(2,1)}) custom-call(bf16[1,1024,2048]{2,1,0:T(8,128)(2,1)} %schur.1, bf16[1024,256]{1,0:T(8,128)(2,1)} %sketch.1, s32[8,64]{1,0:T(8,128)} %block_map.1), custom_call_target="tpu_custom_call" | custom-call | tf_op jit(solution)/shard_map/basis_step/pallas_call | solution.py:526
  110.9 2.1 %results.1 = (f32[2,1,256,256]{3,2,1,0:T(8,128)}, f32[2,1,64,256]{3,2,1,0:T(8,128)}) custom-call(bf16[2,8,128,128]{3,2,1,0:T(8,128)(2,1)} %get-tuple-element.4.basis, bf16[8,2,16,256]{3,2,1,0:T(8,128)(2,1)} %get-tuple-element.5.coupling, s32[32]{0:T(128)} %owner_slot.1), custom_call_target="tpu_custom_call" | custom-call | tf_op jit(solution)/shard_map/results/pallas_call | solution.py:612
